TPU v7x, 256 devices: a whole 4x4x8 slice. The times are simulated.
256 devices in a mesh: chan: 8 (over y, core), row: 32 (over x, z).
Axes of the slice: x: 4, y: 4, z: 8, core: 2. Of those that a mesh axis runs over, the one named last changes fastest.
Arguments:
- voltages: bfloat16 [256, 2, 8, 1024], P('row', None, 'chan'), may hold values from -6 to 6
- kernels: float32 [256, 2, 4], P('row'), may hold values from 0.1 to 1.9
- footprint: int32 [256, 2], P('row'), may hold values from 0 to 252
- cal_weight: float32 [16, 8], P(None, 'chan'), may hold values from -6 to 6
Outputs:
- power_image: float32 [8, 256, 256], P('chan', None, 'row')
- calibrator_maps: float32 [16, 256, 256], P('chan', None, 'row')
All inputs are finite; a program needn't handle non-finite values.
Results may differ from a plain program's by a relative error of at most 0.004.
Values may be sent and summed in bfloat16 or wider, within the bound.
No kernel may reach another device: no remote copies, remote signals or barrier semaphores. Data moves between devices by JAX's collectives and lax.ppermute only.
A program may use at most 128 MiB of HBM per device.

v0:
```python
import math

import jax
import jax.numpy as jnp
from jax import lax
from jax.sharding import PartitionSpec as P

GRID = 256


def dft_tables(size, first, count):
    indices = jnp.arange(size, dtype=jnp.int32)
    columns = first + jnp.arange(count, dtype=jnp.int32)
    phases = indices[:, None] * columns[None, :] % size
    angles = phases.astype(jnp.float32) * (2.0 * math.pi / size)
    return (jnp.cos(angles), jnp.sin(angles))


def placed(weights, starts, count):
    positions = jnp.arange(count, dtype=jnp.int32)
    taps = jnp.arange(weights.shape[1], dtype=jnp.int32)
    target = starts[:, None] + taps[None, :]
    hit = positions[None, None, :] == target[:, :, None]
    return jnp.sum(jnp.where(hit, weights[:, :, None], jnp.zeros((), weights.dtype)), axis=1)


def blocked_time_sum(values):
    samples = values.shape[-1]
    width = math.gcd(samples, 128)
    shaped = values.reshape(values.shape[:-1] + (samples // width, width))
    return jnp.sum(jnp.sum(shaped, axis=-1), axis=-1)


def image_columns(block):
    highest = lax.Precision.HIGHEST
    cos_table, sin_table = dft_tables(block.shape[1], 0, block.shape[1])
    half_real = block[0]
    half_imag = block[1]
    sky_real = jnp.einsum("umx,ul->lmx", half_real, cos_table, precision=highest) + jnp.einsum(
        "umx,ul->lmx", half_imag, sin_table, precision=highest
    )
    sky_imag = jnp.einsum("umx,ul->lmx", half_imag, cos_table, precision=highest) - jnp.einsum(
        "umx,ul->lmx", half_real, sin_table, precision=highest
    )
    return jnp.stack([sky_real, sky_imag])


def on_device(voltages, kernels, footprint, cal_weight):
    highest = lax.Precision.HIGHEST
    local_stations, _, local_channels, samples = voltages.shape
    row_count = lax.axis_size("row")
    grid_size = GRID
    row_share = grid_size // row_count
    first_row = lax.axis_index("row") * row_share
    columns_total = local_channels * samples
    kernel_taps = kernels.shape[2]
    station_count = local_stations * row_count
    power_scale = 1.0 / (2.0 * samples * station_count * kernel_taps * kernel_taps)
    volt_flat = voltages.reshape(local_stations, 2, columns_total)
    volt_all, kern_all, foot_all = (
        lax.all_gather(volt_flat, "row", axis=0, tiled=True),
        lax.all_gather(kernels.astype(jnp.bfloat16), "row", axis=0, tiled=True).astype(
            kernels.dtype
        ),
        lax.all_gather(footprint, "row", axis=0, tiled=True),
    )
    row_weight = placed(kern_all[:, 0, :], foot_all[:, 0], grid_size)
    col_weight = placed(kern_all[:, 1, :], foot_all[:, 1], grid_size)
    cos_local, sin_local = dft_tables(grid_size, first_row, row_share)
    resp_real = jnp.dot(col_weight, cos_local, precision=highest)
    resp_imag = -jnp.dot(col_weight, sin_local, precision=highest)
    volt_values = volt_all.astype(jnp.float32)
    volt_real = volt_values[:, 0, :]
    volt_imag = volt_values[:, 1, :]
    term_real = (
        resp_real[:, :, None] * volt_real[:, None, :]
        - resp_imag[:, :, None] * volt_imag[:, None, :]
    )
    term_imag = (
        resp_real[:, :, None] * volt_imag[:, None, :]
        + resp_imag[:, :, None] * volt_real[:, None, :]
    )
    terms = jnp.stack([term_real, term_imag], axis=1)
    half_image = jnp.einsum("su,skmx->kumx", row_weight, terms, precision=highest)
    sky = image_columns(half_image)
    squared = sky[0] * sky[0] + sky[1] * sky[1]
    squared = squared.reshape(grid_size, row_share, local_channels, samples)
    power_image = jnp.transpose(blocked_time_sum(squared) * power_scale, (2, 0, 1))
    calibrator_maps = lax.psum_scatter(
        jnp.einsum("qc,clm->qlm", cal_weight, power_image, precision=highest),
        "chan",
        scatter_dimension=0,
        tiled=True,
    )
    return (power_image, calibrator_maps)


def solution(mesh):
    placed = (P("row", None, "chan", None), P("row", None, None), P("row", None), P(None, "chan"))
    return jax.shard_map(
        on_device,
        mesh=mesh,
        in_specs=placed,
        out_specs=(P("chan", None, "row"), P("chan", None, "row")),
        check_vma=False,
    )
```

profile of v0, /device:TPU:1, one launch (start us, length us, event | category | flops | bytes accessed | tf_op | source)
XLA Modules:
  0.0 227.0 jit_solution(15883283409992685155)
XLA Ops:
  7.2 0.0 all-gather.4.cloned.1.call-start
  7.2 0.7 all-gather.4.cloned.1.call-update
  7.9 0.0 reduce-scatter.2.cloned.1.call-start
  7.9 0.7 convert_element_type.22
  8.6 0.1 copy.42
  8.7 37.6 %all-gather.1 = s32[32,8,2]{1,2,0:T(2,128)S(1)} all-gather(s32[1,8,2]{1,2,0:T(2,128)} %bitcast.52), channel_id=1, replica_groups=mesh['chan'=8,'row'=32] {'row'}, dimensions={0}, use_global_device_ids=true | all-gather | bytes 2112 | tf_op jit(solution)/shard_map/all_gather | solution.py:65
  46.4 0.1 reshape.103
  46.5 33.6 %all_gather.10 = bf16[256,2,4]{2,1,0:T(2,128)(2,1)S(1)} all-gather(bf16[8,2,4]{2,1,0:T(2,128)(2,1)S(1)} %copy.42), channel_id=1, replica_groups=mesh['chan'=8,'row'=32] {'row'}, dimensions={0}, use_global_device_ids=true | all-gather | bytes 4224 | tf_op jit(solution)/shard_map/all_gather | solution.py:62
  80.1 0.2 fusion.66
  80.3 0.1 copy.46
  80.4 0.1 copy.43
  80.5 0.3 select_reduce_fusion.1
  80.8 0.3 select_reduce_fusion
  81.2 0.8 convolution_negate_fusion
  82.0 0.9 fusion.26
  82.8 2.9 %all-gather.4.cloned.1.call-done = bf16[256,2,1,1024]{3,1,2,0:T(2,128)(2,1)} async-done(((bf16[8,2,1,1024]{3,1,2,0:T(2,128)(2,1)}), bf16[256,2,1,1024]{3,1,2,0:T(2,128)(2,1)}) %all-gather.4.cloned.1.call-update) | async-done | bytes 1048592 | tf_op jit(solution)/shard_map/all_gather | solution.py:61
  85.8 1.9 bitcast_convert_fusion
  87.7 1.6 fusion.65
  89.3 1.1 copy.56
  90.5 1.0 copy.57
  91.4 4.2 %multiply_subtract_fusion = (f32[256,1,8,1024]{0,3,2,1:T(8,128)S(1)}, f32[256,1,8,1024]{0,3,2,1:T(8,128)}) fusion(f32[256,1024]{0,1:T(8,128)S(1)} %bitcast.47, f32[256,8]{0,1:T(8,128)S(1)} %convolution_negate_fusion, f32[256,1024]{0,1:T(8,128)S(1)} %bitcast.46, f32[256,8]{0,1:T(8,128)S(1)} %fusion.26), kind=kLoop, calls=%fused_computation.8 | loop fusion | flops 12582912 | bytes 18890752 | tf_op jit(solution)/shard_map/sub | solution.py:76
  95.7 17.8 %fusion.8 = f32[2,256,8,1024]{1,3,2,0:T(8,128)} fusion(f32[256,1,8,1024]{0,3,2,1:T(8,128)} %get-tuple-element.3, f32[256,1,8,1024]{0,3,2,1:T(8,128)S(1)} %get-tuple-element.2, f32[256,256]{1,0:T(8,128)S(1)} %select_reduce_fusion), kind=kOutput, calls=%fused_computation.13 | convolution fusion | flops 12889096192 | bytes 33816576 | tf_op jit(solution)/shard_map/su,skmx->kumx/dot_general | solution.py:84
  113.5 0.0 copy-start
  113.5 13.4 %fusion.6 = f32[256,8,1024]{2,0,1:T(8,128)S(1)} fusion(f32[2,256,8,1024]{1,3,2,0:T(8,128)} %fusion.8), kind=kOutput, calls=%fused_computation.11 | convolution fusion | flops 6443368448 | bytes 16777216 | tf_op jit(solution)/shard_map/umx,ul->lmx/dot_general | solution.py:42
  126.9 0.0 copy-done
  126.9 11.7 %fusion.4 = f32[256,8,1024]{2,0,1:T(8,128)} fusion(f32[2,256,8,1024]{1,3,2,0:T(8,128)S(1)} %copy-done), kind=kOutput, calls=%fused_computation.9 | convolution fusion | flops 6443368448 | bytes 16777216 | tf_op jit(solution)/shard_map/umx,ul->lmx/dot_general | solution.py:42
  138.7 11.4 %fusion.5 = f32[256,8,1024]{2,0,1:T(8,128)} fusion(f32[2,256,8,1024]{1,3,2,0:T(8,128)S(1)} %copy-done), kind=kOutput, calls=%fused_computation.10 | convolution fusion | flops 6443368448 | bytes 16777216 | tf_op jit(solution)/shard_map/umx,ul->lmx/dot_general | solution.py:39
  150.1 0.0 copy-start.1
  150.1 25.1 %add_reduce_fusion = f32[256,8]{0,1:T(8,128)S(1)} fusion(f32[256,8,1024]{2,0,1:T(8,128)S(1)} %fusion.6, f32[256,8,1024]{2,0,1:T(8,128)} %fusion.4, f32[256,8,1024]{2,0,1:T(8,128)} %fusion.5, f32[2,256,8,1024]{1,3,2,0:T(8,128)} %fusion.8), kind=kOutput, calls=%fused_computation.6 | convolution fusion | flops 6455949312 | bytes 33562624 | tf_op jit(solution)/shard_map/umx,ul->lmx/dot_general | solution.py:39
  175.2 0.6 broadcast_multiply_fusion
  175.8 0.0 copy-done.1
  175.8 0.7 multiply_bitcast_fusion
  176.5 0.0 reduce-scatter.2.cloned.1.call-update
  176.5 43.6 %reduce-scatter.2.cloned.1.call-done = f32[2,256,8]{1,2,0:T(8,128)} async-done(((f32[16,256,8]{1,2,0:T(8,128)}), f32[2,256,8]{1,2,0:T(8,128)}) %reduce-scatter.2.cloned.1.call-update) | async-done | bytes 16400 | tf_op jit(solution)/shard_map/reduce_scatter | solution.py:89
  (5 shorter events, 0.0 us)
Async XLA Ops:
  7.2 78.6 %all-gather.4.cloned.1.call-start = ((), (), s32[]{:S(2)}) async-start(), calls=%async_computation.2 | async-start | bytes 1081344 | tf_op jit(solution)/shard_map/all_gather | solution.py:61
  7.9 212.3 %reduce-scatter.2.cloned.1.call-start = ((), (), s32[]{:S(2)}) async-start(), calls=%async_computation.1 | async-start | bytes 147456 | tf_op jit(solution)/shard_map/reduce_scatter | solution.py:89
  113.5 13.5 %copy-start = (f32[2,256,8,1024]{1,3,2,0:T(8,128)S(1)}, f32[2,256,8,1024]{1,3,2,0:T(8,128)}, u32[]{:S(2)}) copy-start(f32[2,256,8,1024]{1,3,2,0:T(8,128)} %fusion.8) | copy-start | bytes 50331652
  150.1 25.7 %copy-start.1 = (f32[16,1]{0,1:T(1,128)S(1)}, f32[16,1]{0,1:T(1,128)}, u32[]{:S(2)}) copy-start(f32[16,1]{0,1:T(1,128)} %param.7) | copy-start | bytes 196
Sparse Core Ops, SparseCore 0:
  10.6 75.1 all-gather.3
  176.7 43.4 reduce-scatter.1
where the time goes:
time: 229 us; the launch traced here: 227 us
  matrix products  81.1 us (35%)
  blocking collectives  71.3 us (31%)
  waiting for transfers between devices  47.3 us (21%)
  between operations  14.1 us (6%)
  other arithmetic  8.87 us (4%)
  local copies, waits for them, and re-layouts  4.26 us (2%)
    reduce_scatter x1, waiting for transfers between devices, on_device(): lax.psum_scatter(jnp.einsum('qc,clm->qlm', cal_weight, power_image, preci...  43.6 us
    all_gather x1, blocking collectives, on_device(): lax.all_gather(footprint, 'row', axis=0, tiled=True)  37.6 us
    all_gather x1, blocking collectives, on_device(): lax.all_gather(kernels.astype(jnp.bfloat16), 'row', axis=0, tiled=True)  33.6 us
    dot_general x1, matrix products, image_columns(): jnp.einsum('umx,ul->lmx', half_imag, sin_table, precision=highest)  25.1 us
    dot_general x1, matrix products, on_device(): jnp.einsum('su,skmx->kumx', row_weight, terms, precision=highest)  17.8 us
    dot_general x1, matrix products, image_columns(): jnp.einsum('umx,ul->lmx', half_imag, cos_table, precision=highest)  13.4 us
    dot_general x1, matrix products, image_columns(): jnp.einsum('umx,ul->lmx', half_real, sin_table, precision=highest)  11.7 us
    dot_general x1, matrix products, image_columns(): jnp.einsum('umx,ul->lmx', half_real, cos_table, precision=highest)  11.4 us
  transfers between devices with their start and end apart: 2, of which 2 were waited for; matrix products, arithmetic and copies ran while one was open for 2% of the time, Pallas kernels for 0%

commit v1 on v0

v1 whole, which is shorter than its diff:
```python
import functools
import math

import jax
import jax.numpy as jnp
import numpy as np
from jax import lax
from jax.experimental import pallas as pl
from jax.experimental.pallas import tpu as pltpu
from jax.sharding import PartitionSpec as P

GRID = 256
LANES = 128
BF16 = jnp.bfloat16
F32 = jnp.float32


def transform_tables():
    index = np.arange(GRID)
    angles = (index[:, None] * index[None, :] % GRID) * (2.0 * math.pi / GRID)
    exact = np.concatenate([np.cos(angles), np.sin(angles)], axis=1).astype(np.float32)
    high = exact.astype(BF16)
    low = (exact - high.astype(np.float32)).astype(BF16)
    return np.concatenate([high, low], axis=1)


def rounded(values):
    return values.astype(BF16).astype(F32)


def pack_kernel(peers, volt_ref, kern_ref, foot_ref, out_ref, turn_ref):
    stations, _, samples = volt_ref.shape
    taps = kern_ref.shape[1]
    turn_ref[...] = jnp.zeros_like(turn_ref)
    for axis in range(2):
        weights = kern_ref[axis]
        high = rounded(weights)
        turn_ref[axis * taps : (axis + 1) * taps, :stations] = high
        turn_ref[(2 + axis) * taps : (3 + axis) * taps, :stations] = weights - high
    turn_ref[4 * taps : 4 * taps + 2, :stations] = foot_ref[...].astype(F32)
    extra = turn_ref[...].T[:stations].astype(BF16)
    real = volt_ref[:, 0, :]
    imag = volt_ref[:, 1, :]
    for peer in range(peers):
        out_ref[peer, :, :samples] = real
        out_ref[peer, :, samples : 2 * samples] = imag
        out_ref[peer, :, 2 * samples :] = extra


def spread(taps_ref, start, first, count):
    taps = [taps_ref[:, start + k : start + k + 1] for k in range(count)]
    offset = lax.broadcasted_iota(jnp.int32, (first.shape[0], GRID), 1).astype(F32) - first
    out = jnp.zeros_like(offset)
    for k in range(count):
        out = jnp.where(offset == float(k), taps[k], out)
    return out.astype(BF16)


def image_kernel(taps, share, scale, row_of, gathered_ref, tables_ref, weight_ref, power_ref, send_ref,
                 extra_ref, beam_ref, exact_ref):
    stations = gathered_ref.shape[0]
    samples = (gathered_ref.shape[1] - LANES) // 2
    peers = send_ref.shape[0]
    per_peer = weight_ref.shape[0] // peers
    row = row_of()

    both = gathered_ref[:, : 2 * samples]
    real = gathered_ref[:, :samples]
    imag = gathered_ref[:, samples : 2 * samples]
    outer = (((1,), (1,)), ((), ()))
    corr_real = lax.dot_general(both, both, outer, preferred_element_type=F32)
    half = lax.dot_general(imag, real, outer, preferred_element_type=F32)
    corr_imag = half - half.T
    corr_real = corr_real.astype(BF16)
    corr_both = jnp.concatenate([corr_real, (2.0 * corr_imag).astype(BF16)], axis=1)

    extra_ref[...] = gathered_ref[:, 2 * samples :].astype(F32)
    first_row = extra_ref[:, 4 * taps : 4 * taps + 1]
    first_col = extra_ref[:, 4 * taps + 1 : 4 * taps + 2]
    high = jnp.concatenate(
        [spread(extra_ref, 0, first_row, taps), spread(extra_ref, taps, first_col, taps)], axis=0
    )
    low = jnp.concatenate(
        [spread(extra_ref, 2 * taps, first_row, taps), spread(extra_ref, 3 * taps, first_col, taps)],
        axis=0,
    )
    table_high = tables_ref[:, : 2 * GRID]
    table_low = tables_ref[:, 2 * GRID :]
    response = (
        jnp.dot(high, table_high, preferred_element_type=F32)
        + jnp.dot(high, table_low, preferred_element_type=F32)
        + jnp.dot(low, table_high, preferred_element_type=F32)
    )
    row_real = response[:stations, :GRID]
    row_imag = response[:stations, GRID:]
    first = row * share
    upper = first >= LANES
    turn = lax.rem(2 * LANES - first, LANES)
    column = response[stations:]
    col_real = pltpu.roll(
        jnp.where(upper, column[:, LANES : 2 * LANES], column[:, :LANES]), turn, 1
    )
    col_imag = pltpu.roll(
        jnp.where(upper, column[:, 3 * LANES :], column[:, 2 * LANES : 3 * LANES]), turn, 1
    )

    for m in range(share):
        c_real = col_real[:, m : m + 1]
        c_imag = col_imag[:, m : m + 1]
        beam_real = c_real * row_real - c_imag * row_imag
        beam_imag = c_real * row_imag + c_imag * row_real
        exact_ref[m, 0] = beam_real
        exact_ref[m, 1] = beam_imag
        beam_ref[m, :stations] = beam_imag.astype(BF16)
        beam_ref[m, stations:] = beam_real.astype(BF16)
        sum_real = jnp.dot(corr_real, beam_ref[m, stations:], preferred_element_type=F32)
        sum_imag = jnp.dot(corr_both, beam_ref[m], preferred_element_type=F32)
        total = exact_ref[m, 0] * sum_real + exact_ref[m, 1] * sum_imag
        power = jnp.sum(total, axis=0, keepdims=True) * scale
        power_ref[m : m + 1, :] = power
    power = power_ref[...]
    for peer in range(peers):
        for q in range(per_peer):
            send_ref[peer, q * share : (q + 1) * share, :] = power * weight_ref[peer * per_peer + q, 0]


def vmem():
    return pl.BlockSpec(memory_space=pltpu.VMEM)


def packed(volt, kern, foot, peers):
    stations, _, samples = volt.shape
    return pl.pallas_call(
        functools.partial(pack_kernel, peers),
        out_shape=jax.ShapeDtypeStruct((peers, stations, 2 * samples + LANES), BF16),
        in_specs=[vmem()] * 3,
        out_specs=vmem(),
        scratch_shapes=[pltpu.VMEM((LANES, LANES), F32)],
        compiler_params=pltpu.CompilerParams(vmem_limit_bytes=8 << 20),
        name="pack",
    )(volt, kern, foot)


def imaged(gathered, tables, weight, peers, taps, share, scale, row_of, interpret=False):
    stations = gathered.shape[0]
    return pl.pallas_call(
        functools.partial(image_kernel, taps, share, scale, row_of),
        out_shape=(
            jax.ShapeDtypeStruct((share, GRID), F32),
            jax.ShapeDtypeStruct((peers, weight.shape[0] // peers * share, GRID), F32),
        ),
        in_specs=[vmem(), vmem(), pl.BlockSpec(memory_space=pltpu.SMEM)],
        out_specs=(vmem(), vmem()),
        scratch_shapes=[
            pltpu.VMEM((stations, LANES), F32),
            pltpu.VMEM((share, 2 * stations, GRID), BF16),
            pltpu.VMEM((share, 2, stations, GRID), F32),
        ],
        compiler_params=pltpu.CompilerParams(vmem_limit_bytes=24 << 20),
        name="image",
        interpret=interpret,
    )(gathered, tables, weight)


def on_device(tables, voltages, kernels, footprint, cal_weight):
    local_stations, _, local_channels, samples = voltages.shape
    rows = lax.axis_size("row")
    channels = lax.axis_size("chan")
    share = GRID // rows
    taps = kernels.shape[2]
    station_count = local_stations * rows
    scale = 1.0 / (2.0 * samples * station_count * taps * taps)
    volt = voltages.reshape(local_stations, 2, samples)
    send = packed(volt, jnp.transpose(kernels, (1, 2, 0)), footprint.T, rows)
    gathered = lax.all_to_all(send, "row", 0, 0, tiled=True)
    gathered = gathered.reshape(station_count, 2 * samples + LANES)
    power, weighted = imaged(
        gathered, tables, cal_weight, channels, taps, share, scale, lambda: lax.axis_index("row")
    )
    parts = lax.all_to_all(weighted, "chan", 0, 0, tiled=True)
    maps = jnp.sum(parts, axis=0).reshape(-1, share, GRID)
    return jnp.transpose(power[None], (0, 2, 1)), jnp.transpose(maps, (0, 2, 1))


def solution(mesh):
    specs = (P("row", None, "chan", None), P("row", None, None), P("row", None), P(None, "chan"))
    tables = transform_tables()
    return jax.shard_map(
        lambda *args: on_device(jnp.asarray(tables), *args),
        mesh=mesh,
        in_specs=specs,
        out_specs=(P("chan", None, "row"), P("chan", None, "row")),
        check_vma=False,
    )
```

time: 229 us -> 61.6 us (0.27)
  matrix products: 81.1 us -> 0 us
  blocking collectives: 71.3 us -> 14 us
  waiting for transfers between devices: 47.3 us -> 26.4 us
  between operations: 14.1 us -> 0.66 us
  starting transfers between devices: 0.08 us -> 12 us
  other arithmetic: 8.87 us -> 0.62 us
  Pallas kernels: 0 us -> 5.41 us
    dot_general x7 -> x0, matrix products: 81.1 us -> none  [the longest x1 25.1 us: image_columns(): jnp.einsum('umx,ul->lmx', half_imag, sin_table, precision=highest)]
    all_gather x2 -> x0, blocking collectives: 71.3 us -> none  [the longest x1 37.6 us: on_device(): lax.all_gather(footprint, 'row', axis=0, tiled=True)]
    reduce_scatter x1 -> x0, waiting for transfers between devices: 43.6 us -> none  [on_device(): lax.psum_scatter(jnp.einsum('qc,clm->qlm', cal_weight, power_image, preci...]
    all_to_all x0 -> x1, waiting for transfers between devices: none -> 26.4 us  [on_device(): gathered = lax.all_to_all(send, 'row', 0, 0, tiled=True)]
    all_to_all x0 -> x1, blocking collectives: none -> 14 us  [on_device(): parts = lax.all_to_all(weighted, 'chan', 0, 0, tiled=True)]
    all_to_all x0 -> x1, starting transfers between devices: none -> 12 us  [on_device(): gathered = lax.all_to_all(send, 'row', 0, 0, tiled=True)]
    pallas_call x0 -> x2, Pallas kernels: none -> 5.41 us  [the longest x1 4.29 us: imaged(): pl.pallas_call(functools.partial(image_kernel, taps, share, scale, row_of...]
    sub x1 -> x0, other arithmetic: 4.23 us -> none  [on_device(): resp_real[:, :, None] * volt_real[:, None, :]]
  transfers between devices with their start and end apart: 2 -> 1, of which waited for: 2 -> 1; matrix products, arithmetic and copies ran while one was open for 2% -> 0% of each run, Pallas kernels for 0% -> 0%
where the time goes in v1:
time: 61.6 us; the launch traced here: 61.3 us
  waiting for transfers between devices  26.4 us (43%)
  blocking collectives  14 us (23%)
  starting transfers between devices  12 us (19%)
  Pallas kernels  5.41 us (9%)
  local copies, waits for them, and re-layouts  2.21 us (4%)
  between operations  0.66 us (1%)
  other arithmetic  0.62 us (1%)
    all_to_all x1, waiting for transfers between devices, on_device(): gathered = lax.all_to_all(send, 'row', 0, 0, tiled=True)  26.4 us
    all_to_all x1, blocking collectives, on_device(): parts = lax.all_to_all(weighted, 'chan', 0, 0, tiled=True)  14 us
    all_to_all x1, starting transfers between devices, on_device(): gathered = lax.all_to_all(send, 'row', 0, 0, tiled=True)  12 us
    pallas_call x1, Pallas kernels, imaged(): pl.pallas_call(functools.partial(image_kernel, taps, share, scale, row_of...  4.29 us
    unnamed x11, local copies, waits for them, and re-layouts  2.21 us
  transfers between devices with their start and end apart: 1, of which 1 were waited for; matrix products, arithmetic and copies ran while one was open for 0% of the time, Pallas kernels for 0%

profile of v1, /device:TPU:1, one launch (start us, length us, event | category | flops | bytes accessed | tf_op | source)
XLA Modules:
  0.0 61.3 jit_solution(8615680171612405001)
XLA Ops:
  0.6 0.0 copy-start.1
  0.6 0.7 %copy-done.1 = bf16[8,2,1,1024]{3,1,2,0:T(2,128)(2,1)S(1)} copy-done((bf16[8,2,1,1024]{3,1,2,0:T(2,128)(2,1)S(1)}, bf16[8,2,1,1024]{3,1,2,0:T(2,128)(2,1)}, u32[]{:S(2)}) %copy-start.1) | copy-done | bytes 32792
  1.4 0.0 copy-start.2
  1.4 0.7 %copy-done.2 = f32[8,2,4]{0,2,1:T(4,128)S(1)} copy-done((f32[8,2,4]{0,2,1:T(4,128)S(1)}, f32[8,2,4]{0,2,1:T(4,128)}, u32[]{:S(2)}) %copy-start.2) | copy-done | bytes 280
  2.1 0.0 copy-start.3
  2.1 0.7 %copy-done.3 = s32[8,2]{0,1:T(2,128)S(1)} copy-done((s32[8,2]{0,1:T(2,128)S(1)}, s32[8,2]{0,1:T(2,128)}, u32[]{:S(2)}) %copy-start.3) | copy-done | bytes 88
  2.8 1.1 %pack.1 = bf16[32,8,2176]{2,1,0:T(8,128)(2,1)} custom-call(bf16[8,2,1024]{2,1,0:T(2,128)(2,1)S(1)} %bitcast.11, f32[2,4,8]{2,1,0:T(4,128)S(1)} %bitcast.12, s32[2,8]{1,0:T(2,128)S(1)} %bitcast.13), custom_call_target="tpu_custom_call" | custom-call | tf_op jit(solution)/shard_map/pack/pallas_call | solution.py:133
  3.9 0.0 copy-start.4
  3.9 0.0 copy-start
  3.9 12.0 %all-to-all-start = ((bf16[32,8,2176]{2,1,0:T(8,128)(2,1)}), bf16[32,8,2176]{2,1,0:T(8,128)(2,1)S(1)}, u32[]{:S(2)}, u32[]{:S(2)}) async-start(bf16[32,8,2176]{2,1,0:T(8,128)(2,1)} %pack.1), calls=%async_computation | async-start | bytes 2228224 | tf_op jit(solution)/shard_map/all_to_all | solution.py:175
  15.9 0.0 copy-done.4
  15.9 0.1 copy.7.weight_ref
  16.0 26.4 %all-to-all-done = bf16[32,8,2176]{2,1,0:T(8,128)(2,1)S(1)} async-done(((bf16[32,8,2176]{2,1,0:T(8,128)(2,1)}), bf16[32,8,2176]{2,1,0:T(8,128)(2,1)S(1)}, u32[]{:S(2)}, u32[]{:S(2)}) %all-to-all-start) | async-done | bytes 1114144 | tf_op jit(solution)/shard_map/all_to_all | solution.py:175
  42.4 0.0 copy-done
  42.4 4.3 %image.1 = (f32[8,256]{1,0:T(8,128)}, f32[8,16,256]{2,1,0:T(8,128)S(1)}) custom-call(bf16[256,2176]{1,0:T(8,128)(2,1)S(1)} %bitcast.10, bf16[256,1024]{1,0:T(8,128)(2,1)S(1)} %copy-done, f32[16,1]{1,0:T(8,128)S(1)} %copy.7.weight_ref), custom_call_target="tpu_custom_call" | custom-call | tf_op jit(solution)/shard_map/image/pallas_call | solution.py:146
  46.6 14.0 %all_to_all.10 = f32[8,16,256]{2,1,0:T(8,128)S(1)} all-to-all(f32[8,16,256]{2,1,0:T(8,128)S(1)} %get-tuple-element.5), channel_id=1, replica_groups=mesh['chan'=8,'row'=32] {'chan'}, dimensions={0} | all-to-all | bytes 262144 | tf_op jit(solution)/shard_map/all_to_all | solution.py:180
  60.6 0.6 %reduce_sum.9 = f32[16,256]{1,0:T(8,128)} reduce(f32[8,16,256]{2,1,0:T(8,128)S(1)} %all_to_all.10, f32[]{:T(128)} %constant.1.clone.1), dimensions={0}, to_apply=%region_0.0 | reduce | flops 28672 | bytes 147460 | tf_op jit(solution)/shard_map/reduce_sum | solution.py:181
Async XLA Ops:
  0.6 0.8 %copy-start.1 = (bf16[8,2,1,1024]{3,1,2,0:T(2,128)(2,1)S(1)}, bf16[8,2,1,1024]{3,1,2,0:T(2,128)(2,1)}, u32[]{:S(2)}) copy-start(bf16[8,2,1,1024]{3,1,2,0:T(2,128)(2,1)} %param.5) | copy-start | bytes 98308
  1.4 0.7 %copy-start.2 = (f32[8,2,4]{0,2,1:T(4,128)S(1)}, f32[8,2,4]{0,2,1:T(4,128)}, u32[]{:S(2)}) copy-start(f32[8,2,4]{0,2,1:T(4,128)} %param.6) | copy-start | bytes 772
  2.1 0.7 %copy-start.3 = (s32[8,2]{0,1:T(2,128)S(1)}, s32[8,2]{0,1:T(2,128)}, u32[]{:S(2)}) copy-start(s32[8,2]{0,1:T(2,128)} %param.7) | copy-start | bytes 196
  3.9 12.0 %copy-start.4 = (f32[16,1]{0,1:T(1,128)S(1)}, f32[16,1]{0,1:T(1,128)}, u32[]{:S(2)}) copy-start(f32[16,1]{0,1:T(1,128)} %param.8) | copy-start | bytes 196
  3.9 38.5 %copy-start = (bf16[256,1024]{1,0:T(8,128)(2,1)S(1)}, bf16[256,1024]{1,0:T(8,128)(2,1)}, u32[]{:S(2)}) copy-start(bf16[256,1024]{1,0:T(8,128)(2,1)} %constant.4.clone.tables_ref) | copy-start | bytes 1572868
  3.9 38.5 %all-to-all-start = ((bf16[32,8,2176]{2,1,0:T(8,128)(2,1)}), bf16[32,8,2176]{2,1,0:T(8,128)(2,1)S(1)}, u32[]{:S(2)}, u32[]{:S(2)}) async-start(bf16[32,8,2176]{2,1,0:T(8,128)(2,1)} %pack.1), calls=%async_computation | async-start | bytes 2228224 | tf_op jit(solution)/shard_map/all_to_all | solution.py:175

commit v2 on v1

--- a/solution.py
+++ b/solution.py
@@ -28,7 +28,13 @@
     return values.astype(BF16).astype(F32)
 
 
-def pack_kernel(peers, volt_ref, kern_ref, foot_ref, out_ref, turn_ref):
+def pack_kernel(peers, volt_hbm, kern_hbm, foot_hbm, out_ref, turn_ref, volt_ref, kern_ref, foot_ref, sems):
+    sources = ((kern_hbm, kern_ref), (foot_hbm, foot_ref), (volt_hbm, volt_ref))
+    copies = [pltpu.make_async_copy(*pair, sems.at[i]) for i, pair in enumerate(sources)]
+    for copy in copies:
+        copy.start()
+    for copy in copies:
+        copy.wait()
     stations, _, samples = volt_ref.shape
     taps = kern_ref.shape[1]
     turn_ref[...] = jnp.zeros_like(turn_ref)
@@ -61,7 +67,7 @@
     stations = gathered_ref.shape[0]
     samples = (gathered_ref.shape[1] - LANES) // 2
     peers = send_ref.shape[0]
-    per_peer = weight_ref.shape[0] // peers
+    per_peer = weight_ref.shape[1] // peers
     row = row_of()
 
     both = gathered_ref[:, : 2 * samples]
@@ -121,7 +127,7 @@
     power = power_ref[...]
     for peer in range(peers):
         for q in range(per_peer):
-            send_ref[peer, q * share : (q + 1) * share, :] = power * weight_ref[peer * per_peer + q, 0]
+            send_ref[peer, q * share : (q + 1) * share, :] = power * weight_ref[0, peer * per_peer + q]
 
 
 def vmem():
@@ -133,9 +139,11 @@
     return pl.pallas_call(
         functools.partial(pack_kernel, peers),
         out_shape=jax.ShapeDtypeStruct((peers, stations, 2 * samples + LANES), BF16),
-        in_specs=[vmem()] * 3,
+        in_specs=[pl.BlockSpec(memory_space=pltpu.HBM)] * 3,
         out_specs=vmem(),
-        scratch_shapes=[pltpu.VMEM((LANES, LANES), F32)],
+        scratch_shapes=[pltpu.VMEM((LANES, LANES), F32)]
+        + [pltpu.VMEM(x.shape, x.dtype) for x in (volt, kern, foot)]
+        + [pltpu.SemaphoreType.DMA((3,))],
         compiler_params=pltpu.CompilerParams(vmem_limit_bytes=8 << 20),
         name="pack",
     )(volt, kern, foot)
@@ -147,7 +155,7 @@
         functools.partial(image_kernel, taps, share, scale, row_of),
         out_shape=(
             jax.ShapeDtypeStruct((share, GRID), F32),
-            jax.ShapeDtypeStruct((peers, weight.shape[0] // peers * share, GRID), F32),
+            jax.ShapeDtypeStruct((peers, weight.shape[1] // peers * share, GRID), F32),
         ),
         in_specs=[vmem(), vmem(), pl.BlockSpec(memory_space=pltpu.SMEM)],
         out_specs=(vmem(), vmem()),
@@ -175,7 +183,7 @@
     gathered = lax.all_to_all(send, "row", 0, 0, tiled=True)
     gathered = gathered.reshape(station_count, 2 * samples + LANES)
     power, weighted = imaged(
-        gathered, tables, cal_weight, channels, taps, share, scale, lambda: lax.axis_index("row")
+        gathered, tables, cal_weight.T, channels, taps, share, scale, lambda: lax.axis_index("row")
     )
     parts = lax.all_to_all(weighted, "chan", 0, 0, tiled=True)
     maps = jnp.sum(parts, axis=0).reshape(-1, share, GRID)

time: 61.6 us -> 62 us (level)
  blocking collectives: 14 us -> 53.9 us
  waiting for transfers between devices: 26.4 us -> 0 us
  starting transfers between devices: 12 us -> 0 us
  Pallas kernels: 5.41 us -> 4.42 us
    all_to_all x0 -> x1, blocking collectives: none -> 42.4 us  [on_device(): gathered = lax.all_to_all(send, 'row', 0, 0, tiled=True)]
    all_to_all x1 -> x0, waiting for transfers between devices: 26.4 us -> none  [on_device(): gathered = lax.all_to_all(send, 'row', 0, 0, tiled=True)]
    all_to_all x1 -> x0, starting transfers between devices: 12 us -> none  [on_device(): gathered = lax.all_to_all(send, 'row', 0, 0, tiled=True)]
    all_to_all x1, blocking collectives: 14 us -> 11.6 us  [on_device(): parts = lax.all_to_all(weighted, 'chan', 0, 0, tiled=True)]
    pallas_call x1, Pallas kernels: 1.13 us -> 0.25 us  [packed(): pl.pallas_call(functools.partial(pack_kernel, peers), out_shape=jax.Shape...]
    unnamed x11 -> x10, local copies, waits for them, and re-layouts: 2.21 us -> 2.13 us
  transfers between devices with their start and end apart: 1 -> 0, of which waited for: 1 -> 0; matrix products, arithmetic and copies ran while one was open for 0% -> 0% of each run, Pallas kernels for 0% -> 0%
where the time goes in v2:
time: 62 us; the launch traced here: 61.8 us
  blocking collectives  53.9 us (87%)
  Pallas kernels  4.42 us (7%)
  local copies, waits for them, and re-layouts  2.13 us (3%)
  between operations  0.67 us (1%)
  other arithmetic  0.62 us (1%)
    all_to_all x1, blocking collectives, on_device(): gathered = lax.all_to_all(send, 'row', 0, 0, tiled=True)  42.4 us
    all_to_all x1, blocking collectives, on_device(): parts = lax.all_to_all(weighted, 'chan', 0, 0, tiled=True)  11.6 us
    pallas_call x1, Pallas kernels, imaged(): pl.pallas_call(functools.partial(image_kernel, taps, share, scale, row_of...  4.16 us
    unnamed x10, local copies, waits for them, and re-layouts  2.13 us

profile of v2, /device:TPU:1, one launch (start us, length us, event | category | flops | bytes accessed | tf_op | source)
XLA Modules:
  0.0 61.8 jit_solution(481237488777422741)
XLA Ops:
  0.6 0.0 copy-start.1
  0.6 0.7 %copy-done.1 = bf16[8,2,1,1024]{3,1,2,0:T(2,128)(2,1)S(1)} copy-done((bf16[8,2,1,1024]{3,1,2,0:T(2,128)(2,1)S(1)}, bf16[8,2,1,1024]{3,1,2,0:T(2,128)(2,1)}, u32[]{:S(2)}) %copy-start.1) | copy-done | bytes 32792
  1.4 0.0 copy-start.2
  1.4 0.7 %copy-done.2 = f32[8,2,4]{0,2,1:T(4,128)S(1)} copy-done((f32[8,2,4]{0,2,1:T(4,128)S(1)}, f32[8,2,4]{0,2,1:T(4,128)}, u32[]{:S(2)}) %copy-start.2) | copy-done | bytes 280
  2.1 0.0 copy-start.3
  2.1 0.7 %copy-done.3 = s32[8,2]{0,1:T(2,128)S(1)} copy-done((s32[8,2]{0,1:T(2,128)S(1)}, s32[8,2]{0,1:T(2,128)}, u32[]{:S(2)}) %copy-start.3) | copy-done | bytes 88
  2.8 0.3 pack.1
  3.0 0.0 copy-start
  3.0 0.0 copy-start.4
  3.0 42.4 %all_to_all.10 = bf16[32,8,2176]{2,1,0:T(8,128)(2,1)S(1)} all-to-all(bf16[32,8,2176]{2,1,0:T(8,128)(2,1)S(1)} %pack.1), channel_id=1, replica_groups=mesh['chan'=8,'row'=32] {'row'}, dimensions={0} | all-to-all | bytes 2228224 | tf_op jit(solution)/shard_map/all_to_all | solution.py:183
  45.4 0.0 copy-done
  45.4 0.0 copy-done.4
  45.4 4.2 %image.1 = (f32[8,256]{1,0:T(8,128)}, f32[8,16,256]{2,1,0:T(8,128)S(1)}) custom-call(bf16[256,2176]{1,0:T(8,128)(2,1)S(1)} %bitcast.11, bf16[256,1024]{1,0:T(8,128)(2,1)S(1)} %copy-done, f32[1,16]{1,0:T(1,128)S(1)} %bitcast.15), custom_call_target="tpu_custom_call" | custom-call | tf_op jit(solution)/shard_map/image/pallas_call | solution.py:154
  49.6 11.6 %all_to_all.11 = f32[8,16,256]{2,1,0:T(8,128)S(1)} all-to-all(f32[8,16,256]{2,1,0:T(8,128)S(1)} %get-tuple-element.5), channel_id=1, replica_groups=mesh['chan'=8,'row'=32] {'chan'}, dimensions={0} | all-to-all | bytes 262144 | tf_op jit(solution)/shard_map/all_to_all | solution.py:188
  61.1 0.6 reduce_sum.9
Async XLA Ops:
  0.6 0.8 %copy-start.1 = (bf16[8,2,1,1024]{3,1,2,0:T(2,128)(2,1)S(1)}, bf16[8,2,1,1024]{3,1,2,0:T(2,128)(2,1)}, u32[]{:S(2)}) copy-start(bf16[8,2,1,1024]{3,1,2,0:T(2,128)(2,1)} %param.5) | copy-start | bytes 98308
  1.4 0.7 %copy-start.2 = (f32[8,2,4]{0,2,1:T(4,128)S(1)}, f32[8,2,4]{0,2,1:T(4,128)}, u32[]{:S(2)}) copy-start(f32[8,2,4]{0,2,1:T(4,128)} %param.6) | copy-start | bytes 772
  2.1 0.7 %copy-start.3 = (s32[8,2]{0,1:T(2,128)S(1)}, s32[8,2]{0,1:T(2,128)}, u32[]{:S(2)}) copy-start(s32[8,2]{0,1:T(2,128)} %param.7) | copy-start | bytes 196
  3.0 42.4 %copy-start = (bf16[256,1024]{1,0:T(8,128)(2,1)S(1)}, bf16[256,1024]{1,0:T(8,128)(2,1)}, u32[]{:S(2)}) copy-start(bf16[256,1024]{1,0:T(8,128)(2,1)} %constant.4.clone.tables_ref) | copy-start | bytes 1572868
  3.0 42.4 %copy-start.4 = (f32[16,1]{0,1:T(1,128)S(1)}, f32[16,1]{0,1:T(1,128)}, u32[]{:S(2)}) copy-start(f32[16,1]{0,1:T(1,128)} %param.8) | copy-start | bytes 196

commit v3 on v1

--- a/solution.py
+++ b/solution.py
@@ -11,6 +11,7 @@
 
 GRID = 256
 LANES = 128
+SPLIT = 2
 BF16 = jnp.bfloat16
 F32 = jnp.float32
 
@@ -28,23 +29,24 @@
     return values.astype(BF16).astype(F32)
 
 
-def pack_kernel(peers, volt_ref, kern_ref, foot_ref, out_ref, turn_ref):
+def pack_kernel(peers, split, volt_ref, small_ref, out_ref, turn_ref):
     stations, _, samples = volt_ref.shape
-    taps = kern_ref.shape[1]
+    part = samples // split
+    weights = small_ref.shape[0] - 2
     turn_ref[...] = jnp.zeros_like(turn_ref)
-    for axis in range(2):
-        weights = kern_ref[axis]
-        high = rounded(weights)
-        turn_ref[axis * taps : (axis + 1) * taps, :stations] = high
-        turn_ref[(2 + axis) * taps : (3 + axis) * taps, :stations] = weights - high
-    turn_ref[4 * taps : 4 * taps + 2, :stations] = foot_ref[...].astype(F32)
+    values = small_ref[...]
+    high = rounded(values[:weights])
+    turn_ref[:weights, :stations] = high
+    turn_ref[weights : 2 * weights, :stations] = values[:weights] - high
+    turn_ref[2 * weights : 2 * weights + 2, :stations] = values[weights:]
     extra = turn_ref[...].T[:stations].astype(BF16)
     real = volt_ref[:, 0, :]
     imag = volt_ref[:, 1, :]
     for peer in range(peers):
-        out_ref[peer, :, :samples] = real
-        out_ref[peer, :, samples : 2 * samples] = imag
-        out_ref[peer, :, 2 * samples :] = extra
+        start = (peer % split) * part
+        out_ref[peer, :, :part] = real[:, start : start + part]
+        out_ref[peer, :, part : 2 * part] = imag[:, start : start + part]
+        out_ref[peer, :, 2 * part :] = extra
 
 
 def spread(taps_ref, start, first, count):
@@ -56,13 +58,13 @@
     return out.astype(BF16)
 
 
-def image_kernel(taps, share, scale, row_of, gathered_ref, tables_ref, weight_ref, power_ref, send_ref,
-                 extra_ref, beam_ref, exact_ref):
+def image_kernel(taps, share, split, scale, place_of, gathered_ref, tables_ref, weight_ref, send_ref,
+                 extra_ref, beam_ref, exact_ref, power_ref):
     stations = gathered_ref.shape[0]
     samples = (gathered_ref.shape[1] - LANES) // 2
-    peers = send_ref.shape[0]
-    per_peer = weight_ref.shape[0] // peers
-    row = row_of()
+    peers = send_ref.shape[0] // split
+    per_peer = weight_ref.shape[1] // peers
+    channel, row = place_of()
 
     both = gathered_ref[:, : 2 * samples]
     real = gathered_ref[:, :samples]
@@ -93,7 +95,7 @@
     )
     row_real = response[:stations, :GRID]
     row_imag = response[:stations, GRID:]
-    first = row * share
+    first = row // split * (split * share)
     upper = first >= LANES
     turn = lax.rem(2 * LANES - first, LANES)
     column = response[stations:]
@@ -104,7 +106,7 @@
         jnp.where(upper, column[:, 3 * LANES :], column[:, 2 * LANES : 3 * LANES]), turn, 1
     )
 
-    for m in range(share):
+    for m in range(share * split):
         c_real = col_real[:, m : m + 1]
         c_imag = col_imag[:, m : m + 1]
         beam_real = c_real * row_real - c_imag * row_imag
@@ -116,50 +118,87 @@
         sum_real = jnp.dot(corr_real, beam_ref[m, stations:], preferred_element_type=F32)
         sum_imag = jnp.dot(corr_both, beam_ref[m], preferred_element_type=F32)
         total = exact_ref[m, 0] * sum_real + exact_ref[m, 1] * sum_imag
-        power = jnp.sum(total, axis=0, keepdims=True) * scale
-        power_ref[m : m + 1, :] = power
-    power = power_ref[...]
-    for peer in range(peers):
-        for q in range(per_peer):
-            send_ref[peer, q * share : (q + 1) * share, :] = power * weight_ref[peer * per_peer + q, 0]
+        power_ref[m : m + 1, :] = jnp.sum(total, axis=0, keepdims=True) * scale
+    for side in range(split):
+        power = power_ref[side * share : (side + 1) * share, :]
+        for peer in range(peers):
+            for q in range(per_peer):
+                factor = jnp.where(channel == peer, 1.0, weight_ref[0, peer * per_peer + q])
+                send_ref[peer * split + side, q * share : (q + 1) * share, :] = power * factor
+
+
+def finish_kernel(split, channel_of, parts_ref, weight_ref, power_ref, maps_ref):
+    share = power_ref.shape[0]
+    per_peer = maps_ref.shape[0] // share
+    channel = channel_of()
+    peers = parts_ref.shape[0] // split
+    power = jnp.zeros(power_ref.shape, F32)
+    for side in range(split):
+        power += parts_ref[channel * split + side, :share]
+    power_ref[...] = power
+    for q in range(per_peer):
+        total = power * weight_ref[0, channel * per_peer + q]
+        for peer in range(peers):
+            for side in range(split):
+                block = parts_ref[peer * split + side, q * share : (q + 1) * share]
+                total += jnp.where(channel == peer, 0.0, block)
+        maps_ref[q * share : (q + 1) * share] = total
 
 
 def vmem():
     return pl.BlockSpec(memory_space=pltpu.VMEM)
 
 
-def packed(volt, kern, foot, peers):
+def smem():
+    return pl.BlockSpec(memory_space=pltpu.SMEM)
+
+
+def packed(volt, small, peers, split):
     stations, _, samples = volt.shape
     return pl.pallas_call(
-        functools.partial(pack_kernel, peers),
-        out_shape=jax.ShapeDtypeStruct((peers, stations, 2 * samples + LANES), BF16),
-        in_specs=[vmem()] * 3,
+        functools.partial(pack_kernel, peers, split),
+        out_shape=jax.ShapeDtypeStruct((peers, stations, 2 * samples // split + LANES), BF16),
+        in_specs=[vmem()] * 2,
         out_specs=vmem(),
         scratch_shapes=[pltpu.VMEM((LANES, LANES), F32)],
         compiler_params=pltpu.CompilerParams(vmem_limit_bytes=8 << 20),
         name="pack",
-    )(volt, kern, foot)
-
-
-def imaged(gathered, tables, weight, peers, taps, share, scale, row_of, interpret=False):
+    )(volt, small)
+
+
+def imaged(gathered, tables, weight, peers, taps, share, split, scale, place_of, interpret=False):
     stations = gathered.shape[0]
+    columns = share * split
     return pl.pallas_call(
-        functools.partial(image_kernel, taps, share, scale, row_of),
-        out_shape=(
-            jax.ShapeDtypeStruct((share, GRID), F32),
-            jax.ShapeDtypeStruct((peers, weight.shape[0] // peers * share, GRID), F32),
-        ),
-        in_specs=[vmem(), vmem(), pl.BlockSpec(memory_space=pltpu.SMEM)],
-        out_specs=(vmem(), vmem()),
+        functools.partial(image_kernel, taps, share, split, scale, place_of),
+        out_shape=jax.ShapeDtypeStruct((peers * split, weight.shape[1] // peers * share, GRID), F32),
+        in_specs=[vmem(), vmem(), smem()],
+        out_specs=vmem(),
         scratch_shapes=[
             pltpu.VMEM((stations, LANES), F32),
-            pltpu.VMEM((share, 2 * stations, GRID), BF16),
-            pltpu.VMEM((share, 2, stations, GRID), F32),
+            pltpu.VMEM((columns, 2 * stations, GRID), BF16),
+            pltpu.VMEM((columns, 2, stations, GRID), F32),
+            pltpu.VMEM((columns, GRID), F32),
         ],
-        compiler_params=pltpu.CompilerParams(vmem_limit_bytes=24 << 20),
+        compiler_params=pltpu.CompilerParams(vmem_limit_bytes=32 << 20),
         name="image",
         interpret=interpret,
     )(gathered, tables, weight)
+
+
+def finished(parts, weight, share, split, channel_of, interpret=False):
+    return pl.pallas_call(
+        functools.partial(finish_kernel, split, channel_of),
+        out_shape=(
+            jax.ShapeDtypeStruct((share, GRID), F32),
+            jax.ShapeDtypeStruct((parts.shape[1], GRID), F32),
+        ),
+        in_specs=[vmem(), smem()],
+        out_specs=(vmem(), vmem()),
+        compiler_params=pltpu.CompilerParams(vmem_limit_bytes=8 << 20),
+        name="finish",
+        interpret=interpret,
+    )(parts, weight)
 
 
 def on_device(tables, voltages, kernels, footprint, cal_weight):
@@ -171,14 +210,26 @@
     station_count = local_stations * rows
     scale = 1.0 / (2.0 * samples * station_count * taps * taps)
     volt = voltages.reshape(local_stations, 2, samples)
-    send = packed(volt, jnp.transpose(kernels, (1, 2, 0)), footprint.T, rows)
+    small = jnp.concatenate(
+        [jnp.transpose(kernels, (1, 2, 0)).reshape(2 * taps, -1), footprint.T.astype(F32)], axis=0
+    )
+    send = packed(volt, small, rows, SPLIT)
     gathered = lax.all_to_all(send, "row", 0, 0, tiled=True)
-    gathered = gathered.reshape(station_count, 2 * samples + LANES)
-    power, weighted = imaged(
-        gathered, tables, cal_weight, channels, taps, share, scale, lambda: lax.axis_index("row")
-    )
-    parts = lax.all_to_all(weighted, "chan", 0, 0, tiled=True)
-    maps = jnp.sum(parts, axis=0).reshape(-1, share, GRID)
+    gathered = gathered.reshape(station_count, -1)
+    weight = cal_weight.T
+    weighted = imaged(
+        gathered, tables, weight, channels, taps, share, SPLIT, scale,
+        lambda: (lax.axis_index("chan"), lax.axis_index("row")),
+    )
+    groups = [
+        [c * rows + first + side for c in range(channels) for side in range(SPLIT)]
+        for first in range(0, rows, SPLIT)
+    ]
+    parts = lax.all_to_all(
+        weighted, ("chan", "row"), 0, 0, axis_index_groups=groups, tiled=True
+    )
+    power, maps = finished(parts, weight, share, SPLIT, lambda: lax.axis_index("chan"))
+    maps = maps.reshape(-1, share, GRID)
     return jnp.transpose(power[None], (0, 2, 1)), jnp.transpose(maps, (0, 2, 1))
 
 

time: 61.6 us -> 53.9 us (0.88)
  blocking collectives: 14 us -> 44.4 us
  waiting for transfers between devices: 26.4 us -> 0 us
  starting transfers between devices: 12 us -> 0 us
  local copies, waits for them, and re-layouts: 2.21 us -> 1.42 us
  other arithmetic: 0.62 us -> 1.37 us
    all_to_all x1 -> x2, blocking collectives: 14 us -> 44.4 us  [the longest x1 27.2 us: on_device(): gathered = lax.all_to_all(send, 'row', 0, 0, tiled=True)]
    all_to_all x1 -> x0, waiting for transfers between devices: 26.4 us -> none  [on_device(): gathered = lax.all_to_all(send, 'row', 0, 0, tiled=True)]
    all_to_all x1 -> x0, starting transfers between devices: 12 us -> none  [on_device(): gathered = lax.all_to_all(send, 'row', 0, 0, tiled=True)]
    unnamed x11 -> x6, local copies, waits for them, and re-layouts: 2.21 us -> 1.42 us
    concatenate x0 -> x1, other arithmetic: none -> 0.69 us  [on_device(): jnp.concatenate([jnp.transpose(kernels, (1, 2, 0)).reshape(2 * taps, -1),...]
    convert_element_type x0 -> x1, other arithmetic: none -> 0.68 us  [on_device(): footprint.T.astype(F32)]
    reduce_sum x1 -> x0, other arithmetic: 0.62 us -> none  [on_device(): maps = jnp.sum(parts, axis=0).reshape(-1, share, GRID)]
    pallas_call x2 -> x3, Pallas kernels: 5.41 us -> 5.82 us  [the longest x1 4.54 us: imaged(): pl.pallas_call(functools.partial(image_kernel, taps, share, split, scale,...]
  transfers between devices with their start and end apart: 1 -> 0, of which waited for: 1 -> 0; matrix products, arithmetic and copies ran while one was open for 0% -> 0% of each run, Pallas kernels for 0% -> 0%
where the time goes in v3:
time: 53.9 us; the launch traced here: 53.7 us
  blocking collectives  44.4 us (82%)
  Pallas kernels  5.82 us (11%)
  local copies, waits for them, and re-layouts  1.42 us (3%)
  other arithmetic  1.37 us (3%)
  between operations  0.65 us (1%)
    all_to_all x1, blocking collectives, on_device(): gathered = lax.all_to_all(send, 'row', 0, 0, tiled=True)  27.2 us
    all_to_all x1, blocking collectives, on_device(): lax.all_to_all(weighted, ('chan', 'row'), 0, 0, axis_index_groups=groups,...  17.2 us
    pallas_call x1, Pallas kernels, imaged(): pl.pallas_call(functools.partial(image_kernel, taps, share, split, scale,...  4.54 us
    unnamed x6, local copies, waits for them, and re-layouts  1.42 us
    pallas_call x1, Pallas kernels, finished(): pl.pallas_call(functools.partial(finish_kernel, split, channel_of), out_s...  1.18 us

profile of v3, /device:TPU:1, one launch (start us, length us, event | category | flops | bytes accessed | tf_op | source)
XLA Modules:
  0.0 53.7 jit_solution(9890560890634617887)
XLA Ops:
  0.6 0.7 %convert_bitcast_fusion = f32[2,8]{1,0:T(2,128)S(1)} fusion(s32[8,2]{0,1:T(2,128)} %param.7), kind=kLoop, calls=%fused_computation.1 | loop fusion | flops 16 | bytes 128 | tf_op jit(solution)/shard_map/convert_element_type | solution.py:214
  1.3 0.7 %pad_maximum_fusion.small_ref = f32[10,8]{1,0:T(8,128)S(1)} fusion(f32[2,8]{1,0:T(2,128)S(1)} %convert_bitcast_fusion, f32[8,8]{1,0:T(8,128)} %bitcast.18), kind=kLoop, calls=%fused_computation | loop fusion | flops 80 | bytes 640 | tf_op jit(solution)/shard_map/concatenate | solution.py:213
  2.0 0.0 copy-start.1
  2.0 0.8 %copy-done.1 = bf16[8,2,1,1024]{3,1,2,0:T(2,128)(2,1)S(1)} copy-done((bf16[8,2,1,1024]{3,1,2,0:T(2,128)(2,1)S(1)}, bf16[8,2,1,1024]{3,1,2,0:T(2,128)(2,1)}, u32[]{:S(2)}) %copy-start.1) | copy-done | bytes 32792
  2.8 0.1 pack.1
  2.9 0.0 copy-start
  2.9 27.2 %all_to_all.10 = bf16[32,8,1152]{2,1,0:T(8,128)(2,1)S(1)} all-to-all(bf16[32,8,1152]{2,1,0:T(8,128)(2,1)S(1)} %pack.1), channel_id=1, replica_groups=mesh['chan'=8,'row'=32] {'row'}, dimensions={0} | all-to-all | bytes 1179648 | tf_op jit(solution)/shard_map/all_to_all | solution.py:217
  30.0 0.0 copy-start.2
  30.1 0.0 copy-done
  30.1 0.7 %copy-done.2 = f32[16,1]{0,1:T(1,128)S(1)} copy-done((f32[16,1]{0,1:T(1,128)S(1)}, f32[16,1]{0,1:T(1,128)}, u32[]{:S(2)}) %copy-start.2) | copy-done | bytes 88
  30.7 4.5 %image.1 = f32[16,16,256]{2,1,0:T(8,128)S(1)} custom-call(bf16[256,1152]{1,0:T(8,128)(2,1)S(1)} %bitcast.14, bf16[256,1024]{1,0:T(8,128)(2,1)S(1)} %copy-done, f32[1,16]{1,0:T(1,128)S(1)} %bitcast.16), custom_call_target="tpu_custom_call" | custom-call | tf_op jit(solution)/shard_map/image/pallas_call | solution.py:172
  35.3 17.2 %all_to_all.11.parts_ref = f32[16,16,256]{2,1,0:T(8,128)S(1)} all-to-all(f32[16,16,256]{2,1,0:T(8,128)S(1)} %image.1), channel_id=1, replica_groups={{0,1,32,33,64,65,96,97,128,129,160,161,192,193,224,225},{2,3,34,35,66,6..., dimensions={0} | all-to-all | bytes 524288 | tf_op jit(solution)/shard_map/all_to_all | solution.py:228
  52.5 1.2 %finish.1 = (f32[8,256]{1,0:T(8,128)}, f32[16,256]{1,0:T(8,128)}) custom-call(f32[16,16,256]{2,1,0:T(8,128)S(1)} %all_to_all.11.parts_ref, f32[1,16]{1,0:T(1,128)S(1)} %bitcast.17), custom_call_target="tpu_custom_call" | custom-call | tf_op jit(solution)/shard_map/finish/pallas_call | solution.py:190
Async XLA Ops:
  2.0 0.8 %copy-start.1 = (bf16[8,2,1,1024]{3,1,2,0:T(2,128)(2,1)S(1)}, bf16[8,2,1,1024]{3,1,2,0:T(2,128)(2,1)}, u32[]{:S(2)}) copy-start(bf16[8,2,1,1024]{3,1,2,0:T(2,128)(2,1)} %param.5) | copy-start | bytes 98308
  2.9 27.2 %copy-start = (bf16[256,1024]{1,0:T(8,128)(2,1)S(1)}, bf16[256,1024]{1,0:T(8,128)(2,1)}, u32[]{:S(2)}) copy-start(bf16[256,1024]{1,0:T(8,128)(2,1)} %constant.2.clone.tables_ref) | copy-start | bytes 1572868
  30.0 0.7 %copy-start.2 = (f32[16,1]{0,1:T(1,128)S(1)}, f32[16,1]{0,1:T(1,128)}, u32[]{:S(2)}) copy-start(f32[16,1]{0,1:T(1,128)} %param.8) | copy-start | bytes 196

commit v4 on v3

--- a/solution.py
+++ b/solution.py
@@ -29,16 +29,24 @@
     return values.astype(BF16).astype(F32)
 
 
-def pack_kernel(peers, split, volt_ref, small_ref, out_ref, turn_ref):
+def pack_kernel(peers, split, volt_hbm, kern_hbm, foot_hbm, gain_hbm, out_ref, weight_ref,
+                turn_ref, volt_ref, kern_ref, foot_ref, sems):
+    pairs = ((kern_hbm, kern_ref), (foot_hbm, foot_ref), (gain_hbm, weight_ref), (volt_hbm, volt_ref))
+    copies = [pltpu.make_async_copy(*pair, sems.at[i]) for i, pair in enumerate(pairs)]
+    for copy in copies:
+        copy.start()
     stations, _, samples = volt_ref.shape
     part = samples // split
-    weights = small_ref.shape[0] - 2
+    taps = kern_ref.shape[1]
     turn_ref[...] = jnp.zeros_like(turn_ref)
-    values = small_ref[...]
-    high = rounded(values[:weights])
-    turn_ref[:weights, :stations] = high
-    turn_ref[weights : 2 * weights, :stations] = values[:weights] - high
-    turn_ref[2 * weights : 2 * weights + 2, :stations] = values[weights:]
+    for copy in copies:
+        copy.wait()
+    for axis in range(2):
+        values = kern_ref[axis]
+        high = rounded(values)
+        turn_ref[axis * taps : (axis + 1) * taps, :stations] = high
+        turn_ref[(2 + axis) * taps : (3 + axis) * taps, :stations] = values - high
+    turn_ref[4 * taps : 4 * taps + 2, :stations] = foot_ref[...].astype(F32)
     extra = turn_ref[...].T[:stations].astype(BF16)
     real = volt_ref[:, 0, :]
     imag = volt_ref[:, 1, :]
@@ -58,21 +66,21 @@
     return out.astype(BF16)
 
 
-def image_kernel(taps, share, split, scale, place_of, gathered_ref, tables_ref, weight_ref, send_ref,
+def image_kernel(taps, share, split, scale, row_of, gathered_ref, tables_ref, weight_ref, send_ref,
                  extra_ref, beam_ref, exact_ref, power_ref):
     stations = gathered_ref.shape[0]
     samples = (gathered_ref.shape[1] - LANES) // 2
     peers = send_ref.shape[0] // split
     per_peer = weight_ref.shape[1] // peers
-    channel, row = place_of()
+    row = row_of()
 
     both = gathered_ref[:, : 2 * samples]
     real = gathered_ref[:, :samples]
     imag = gathered_ref[:, samples : 2 * samples]
     outer = (((1,), (1,)), ((), ()))
     corr_real = lax.dot_general(both, both, outer, preferred_element_type=F32)
-    half = lax.dot_general(imag, real, outer, preferred_element_type=F32)
-    corr_imag = half - half.T
+    corr_imag = lax.dot_general(imag, real, outer, preferred_element_type=F32)
+    corr_imag -= lax.dot_general(real, imag, outer, preferred_element_type=F32)
     corr_real = corr_real.astype(BF16)
     corr_both = jnp.concatenate([corr_real, (2.0 * corr_imag).astype(BF16)], axis=1)
 
@@ -119,60 +127,70 @@
         sum_imag = jnp.dot(corr_both, beam_ref[m], preferred_element_type=F32)
         total = exact_ref[m, 0] * sum_real + exact_ref[m, 1] * sum_imag
         power_ref[m : m + 1, :] = jnp.sum(total, axis=0, keepdims=True) * scale
-    for side in range(split):
-        power = power_ref[side * share : (side + 1) * share, :]
-        for peer in range(peers):
-            for q in range(per_peer):
-                factor = jnp.where(channel == peer, 1.0, weight_ref[0, peer * per_peer + q])
-                send_ref[peer * split + side, q * share : (q + 1) * share, :] = power * factor
-
-
-def finish_kernel(split, channel_of, parts_ref, weight_ref, power_ref, maps_ref):
+    weights = weight_ref[...]
+    for peer in range(peers):
+        own = weights[:, peer * per_peer : (peer + 1) * per_peer]
+        own = jnp.concatenate([own, jnp.zeros((1, LANES - per_peer), F32)], axis=1)
+        for side in range(split):
+            block = peer * split + side
+            for m in range(share):
+                column = side * share + m
+                send_ref[block, :, m * GRID : (m + 1) * GRID] = power_ref[column : column + 1, :]
+            send_ref[block, :, share * GRID :] = own
+
+
+def finish_kernel(split, channel_of, parts_ref, power_ref, maps_ref):
     share = power_ref.shape[0]
     per_peer = maps_ref.shape[0] // share
     channel = channel_of()
-    peers = parts_ref.shape[0] // split
-    power = jnp.zeros(power_ref.shape, F32)
-    for side in range(split):
-        power += parts_ref[channel * split + side, :share]
-    power_ref[...] = power
-    for q in range(per_peer):
-        total = power * weight_ref[0, channel * per_peer + q]
-        for peer in range(peers):
-            for side in range(split):
-                block = parts_ref[peer * split + side, q * share : (q + 1) * share]
-                total += jnp.where(channel == peer, 0.0, block)
-        maps_ref[q * share : (q + 1) * share] = total
+    blocks = parts_ref.shape[0]
+    parts = parts_ref[:, 0, :]
+    source = lax.broadcasted_iota(jnp.int32, (blocks, 1), 0) // split
+    mask = jnp.where(source == channel, 1.0, 0.0)
+    weights = parts[:, share * GRID :]
+    factors = [mask] + [weights[:, q : q + 1] for q in range(per_peer)]
+    for m in range(share):
+        block = parts[:, m * GRID : (m + 1) * GRID]
+        power_ref[m : m + 1, :] = jnp.sum(block * factors[0], axis=0, keepdims=True)
+        for q in range(per_peer):
+            place = q * share + m
+            maps_ref[place : place + 1, :] = jnp.sum(block * factors[1 + q], axis=0, keepdims=True)
 
 
 def vmem():
     return pl.BlockSpec(memory_space=pltpu.VMEM)
 
 
-def smem():
-    return pl.BlockSpec(memory_space=pltpu.SMEM)
-
-
-def packed(volt, small, peers, split):
+def packed(volt, kern, foot, gain, peers, split):
     stations, _, samples = volt.shape
+    inputs = [pltpu.with_memory_space_constraint(x, pltpu.HBM) for x in (volt, kern, foot, gain)]
     return pl.pallas_call(
         functools.partial(pack_kernel, peers, split),
-        out_shape=jax.ShapeDtypeStruct((peers, stations, 2 * samples // split + LANES), BF16),
-        in_specs=[vmem()] * 2,
-        out_specs=vmem(),
-        scratch_shapes=[pltpu.VMEM((LANES, LANES), F32)],
+        out_shape=(
+            jax.ShapeDtypeStruct((peers, stations, 2 * samples // split + LANES), BF16),
+            jax.ShapeDtypeStruct(gain.shape, F32),
+        ),
+        in_specs=[pl.BlockSpec(memory_space=pltpu.HBM)] * 4,
+        out_specs=(vmem(), vmem()),
+        scratch_shapes=[
+            pltpu.VMEM((LANES, LANES), F32),
+            pltpu.VMEM(volt.shape, volt.dtype),
+            pltpu.VMEM(kern.shape, kern.dtype),
+            pltpu.VMEM(foot.shape, foot.dtype),
+            pltpu.SemaphoreType.DMA((4,)),
+        ],
         compiler_params=pltpu.CompilerParams(vmem_limit_bytes=8 << 20),
         name="pack",
-    )(volt, small)
-
-
-def imaged(gathered, tables, weight, peers, taps, share, split, scale, place_of, interpret=False):
+    )(*inputs)
+
+
+def imaged(gathered, tables, weight, peers, taps, share, split, scale, row_of, interpret=False):
     stations = gathered.shape[0]
     columns = share * split
     return pl.pallas_call(
-        functools.partial(image_kernel, taps, share, split, scale, place_of),
-        out_shape=jax.ShapeDtypeStruct((peers * split, weight.shape[1] // peers * share, GRID), F32),
-        in_specs=[vmem(), vmem(), smem()],
+        functools.partial(image_kernel, taps, share, split, scale, row_of),
+        out_shape=jax.ShapeDtypeStruct((peers * split, 1, share * GRID + LANES), F32),
+        in_specs=[vmem()] * 3,
         out_specs=vmem(),
         scratch_shapes=[
             pltpu.VMEM((stations, LANES), F32),
@@ -186,19 +204,19 @@
     )(gathered, tables, weight)
 
 
-def finished(parts, weight, share, split, channel_of, interpret=False):
+def finished(parts, share, per_peer, split, channel_of, interpret=False):
     return pl.pallas_call(
         functools.partial(finish_kernel, split, channel_of),
         out_shape=(
             jax.ShapeDtypeStruct((share, GRID), F32),
-            jax.ShapeDtypeStruct((parts.shape[1], GRID), F32),
+            jax.ShapeDtypeStruct((per_peer * share, GRID), F32),
         ),
-        in_specs=[vmem(), smem()],
+        in_specs=[vmem()],
         out_specs=(vmem(), vmem()),
         compiler_params=pltpu.CompilerParams(vmem_limit_bytes=8 << 20),
         name="finish",
         interpret=interpret,
-    )(parts, weight)
+    )(parts)
 
 
 def on_device(tables, voltages, kernels, footprint, cal_weight):
@@ -210,16 +228,13 @@
     station_count = local_stations * rows
     scale = 1.0 / (2.0 * samples * station_count * taps * taps)
     volt = voltages.reshape(local_stations, 2, samples)
-    small = jnp.concatenate(
-        [jnp.transpose(kernels, (1, 2, 0)).reshape(2 * taps, -1), footprint.T.astype(F32)], axis=0
-    )
-    send = packed(volt, small, rows, SPLIT)
+    kern = jnp.transpose(kernels, (1, 2, 0))
+    send, weight = packed(volt, kern, footprint.T, cal_weight.T, rows, SPLIT)
     gathered = lax.all_to_all(send, "row", 0, 0, tiled=True)
     gathered = gathered.reshape(station_count, -1)
-    weight = cal_weight.T
     weighted = imaged(
         gathered, tables, weight, channels, taps, share, SPLIT, scale,
-        lambda: (lax.axis_index("chan"), lax.axis_index("row")),
+        lambda: lax.axis_index("row"),
     )
     groups = [
         [c * rows + first + side for c in range(channels) for side in range(SPLIT)]
@@ -228,7 +243,7 @@
     parts = lax.all_to_all(
         weighted, ("chan", "row"), 0, 0, axis_index_groups=groups, tiled=True
     )
-    power, maps = finished(parts, weight, share, SPLIT, lambda: lax.axis_index("chan"))
+    power, maps = finished(parts, share, weight.shape[1] // channels, SPLIT, lambda: lax.axis_index("chan"))
     maps = maps.reshape(-1, share, GRID)
     return jnp.transpose(power[None], (0, 2, 1)), jnp.transpose(maps, (0, 2, 1))
 

time: 53.9 us -> 50.5 us (0.937)
  local copies, waits for them, and re-layouts: 1.42 us -> 0.01 us
  other arithmetic: 1.37 us -> 0 us
  blocking collectives: 44.4 us -> 43.5 us
    unnamed x6 -> x2, local copies, waits for them, and re-layouts: 1.42 us -> 0.01 us
    pallas_call x1, Pallas kernels: 0.1 us -> 1 us  [packed(): pl.pallas_call(functools.partial(pack_kernel, peers, split), out_shape=(j...]
    all_to_all x1, blocking collectives: 17.2 us -> 16.3 us  [on_device(): lax.all_to_all(weighted, ('chan', 'row'), 0, 0, axis_index_groups=groups,...]
    concatenate x1 -> x0, other arithmetic: 0.69 us -> none  [on_device(): jnp.concatenate([jnp.transpose(kernels, (1, 2, 0)).reshape(2 * taps, -1),...]
    convert_element_type x1 -> x0, other arithmetic: 0.68 us -> none  [on_device(): footprint.T.astype(F32)]
where the time goes in v4:
time: 50.5 us; the launch traced here: 50.3 us
  blocking collectives  43.5 us (86%)
  Pallas kernels  6.08 us (12%)
  between operations  0.65 us (1%)
    all_to_all x1, blocking collectives, on_device(): gathered = lax.all_to_all(send, 'row', 0, 0, tiled=True)  27.2 us
    all_to_all x1, blocking collectives, on_device(): lax.all_to_all(weighted, ('chan', 'row'), 0, 0, axis_index_groups=groups,...  16.3 us
    pallas_call x1, Pallas kernels, imaged(): pl.pallas_call(functools.partial(image_kernel, taps, share, split, scale,...  4.18 us

profile of v4, /device:TPU:1, one launch (start us, length us, event | category | flops | bytes accessed | tf_op | source)
XLA Modules:
  0.0 50.3 jit_solution(3857656335111987778)
XLA Ops:
  0.6 1.0 %pack.1 = (bf16[32,8,1152]{2,1,0:T(8,128)(2,1)S(1)}, f32[1,16]{1,0:T(1,128)S(1)}) custom-call(bf16[8,2,1024]{2,1,0:T(2,128)(2,1)} %bitcast.12, f32[2,4,8]{2,1,0:T(4,128)} %bitcast.13, s32[2,8]{1,0:T(2,128)} %bitcast.14, f32[1,16]{1,0:T(1,128)} %bitcast.15), custom_call_target="tpu_custom_call" | custom-call | tf_op jit(solution)/shard_map/pack/pallas_call | solution.py:167
  1.6 0.0 copy-start
  1.7 27.2 %all_to_all.10 = bf16[32,8,1152]{2,1,0:T(8,128)(2,1)S(1)} all-to-all(bf16[32,8,1152]{2,1,0:T(8,128)(2,1)S(1)} %get-tuple-element.6), channel_id=1, replica_groups=mesh['chan'=8,'row'=32] {'row'}, dimensions={0} | all-to-all | bytes 1179648 | tf_op jit(solution)/shard_map/all_to_all | solution.py:233
  28.8 0.0 copy-done
  28.8 4.2 %image.1 = f32[16,1,2176]{2,1,0:T(1,128)S(1)} custom-call(bf16[256,1152]{1,0:T(8,128)(2,1)S(1)} %bitcast.11, bf16[256,1024]{1,0:T(8,128)(2,1)S(1)} %copy-done, f32[1,16]{1,0:T(1,128)S(1)} %get-tuple-element.7.weight_ref), custom_call_target="tpu_custom_call" | custom-call | tf_op jit(solution)/shard_map/image/pallas_call | solution.py:190
  33.0 16.3 %all_to_all.11.parts_ref = f32[16,1,2176]{2,1,0:T(1,128)S(1)} all-to-all(f32[16,1,2176]{2,1,0:T(1,128)S(1)} %image.1), channel_id=1, replica_groups={{0,1,32,33,64,65,96,97,128,129,160,161,192,193,224,225},{2,3,34,35,66,6..., dimensions={0} | all-to-all | bytes 278528 | tf_op jit(solution)/shard_map/all_to_all | solution.py:243
  49.4 0.9 %finish.1 = (f32[8,256]{1,0:T(8,128)}, f32[16,256]{1,0:T(8,128)}) custom-call(f32[16,1,2176]{2,1,0:T(1,128)S(1)} %all_to_all.11.parts_ref), custom_call_target="tpu_custom_call" | custom-call | tf_op jit(solution)/shard_map/finish/pallas_call | solution.py:208
Async XLA Ops:
  1.6 27.2 %copy-start = (bf16[256,1024]{1,0:T(8,128)(2,1)S(1)}, bf16[256,1024]{1,0:T(8,128)(2,1)}, u32[]{:S(2)}) copy-start(bf16[256,1024]{1,0:T(8,128)(2,1)} %constant.2.clone.tables_ref) | copy-start | bytes 1572868

commit v5 on v4

--- a/solution.py
+++ b/solution.py
@@ -12,6 +12,7 @@
 GRID = 256
 LANES = 128
 SPLIT = 2
+GROUP = 2
 BF16 = jnp.bfloat16
 F32 = jnp.float32
 
@@ -19,7 +20,7 @@
 def transform_tables():
     index = np.arange(GRID)
     angles = (index[:, None] * index[None, :] % GRID) * (2.0 * math.pi / GRID)
-    exact = np.concatenate([np.cos(angles), np.sin(angles)], axis=1).astype(np.float32)
+    exact = np.concatenate([np.cos(angles), np.sin(angles)], axis=0).astype(np.float32)
     high = exact.astype(BF16)
     low = (exact - high.astype(np.float32)).astype(BF16)
     return np.concatenate([high, low], axis=1)
@@ -57,76 +58,86 @@
         out_ref[peer, :, 2 * part :] = extra
 
 
-def spread(taps_ref, start, first, count):
-    taps = [taps_ref[:, start + k : start + k + 1] for k in range(count)]
-    offset = lax.broadcasted_iota(jnp.int32, (first.shape[0], GRID), 1).astype(F32) - first
-    out = jnp.zeros_like(offset)
-    for k in range(count):
-        out = jnp.where(offset == float(k), taps[k], out)
-    return out.astype(BF16)
+def spread(first, high, low):
+    offset = lax.broadcasted_iota(jnp.int32, (GRID, first.shape[1]), 0).astype(F32) - first
+    offset = offset.astype(BF16)
+    high, low = high.astype(BF16), low.astype(BF16)
+    out_high = jnp.zeros_like(offset)
+    out_low = jnp.zeros_like(offset)
+    for k in range(high.shape[0]):
+        hit = offset == jnp.asarray(k, BF16)
+        out_high = jnp.where(hit, high[k : k + 1], out_high)
+        out_low = jnp.where(hit, low[k : k + 1], out_low)
+    return out_high, out_low
+
+
+def respond(table, high, low):
+    return (
+        jnp.dot(table[:, :GRID], high, preferred_element_type=F32)
+        + jnp.dot(table[:, GRID:], high, preferred_element_type=F32)
+        + jnp.dot(table[:, :GRID], low, preferred_element_type=F32)
+    )
 
 
 def image_kernel(taps, share, split, scale, row_of, gathered_ref, tables_ref, weight_ref, send_ref,
-                 extra_ref, beam_ref, exact_ref, power_ref):
+                 corr_ref, rows_ref, beam_a, beam_b, exact_a, exact_b, column_ref):
     stations = gathered_ref.shape[0]
     samples = (gathered_ref.shape[1] - LANES) // 2
     peers = send_ref.shape[0] // split
     per_peer = weight_ref.shape[1] // peers
+    columns = share * split
     row = row_of()
 
     both = gathered_ref[:, : 2 * samples]
     real = gathered_ref[:, :samples]
     imag = gathered_ref[:, samples : 2 * samples]
     outer = (((1,), (1,)), ((), ()))
-    corr_real = lax.dot_general(both, both, outer, preferred_element_type=F32)
-    corr_imag = lax.dot_general(imag, real, outer, preferred_element_type=F32)
-    corr_imag -= lax.dot_general(real, imag, outer, preferred_element_type=F32)
-    corr_real = corr_real.astype(BF16)
-    corr_both = jnp.concatenate([corr_real, (2.0 * corr_imag).astype(BF16)], axis=1)
-
-    extra_ref[...] = gathered_ref[:, 2 * samples :].astype(F32)
-    first_row = extra_ref[:, 4 * taps : 4 * taps + 1]
-    first_col = extra_ref[:, 4 * taps + 1 : 4 * taps + 2]
-    high = jnp.concatenate(
-        [spread(extra_ref, 0, first_row, taps), spread(extra_ref, taps, first_col, taps)], axis=0
-    )
-    low = jnp.concatenate(
-        [spread(extra_ref, 2 * taps, first_row, taps), spread(extra_ref, 3 * taps, first_col, taps)],
-        axis=0,
-    )
-    table_high = tables_ref[:, : 2 * GRID]
-    table_low = tables_ref[:, 2 * GRID :]
-    response = (
-        jnp.dot(high, table_high, preferred_element_type=F32)
-        + jnp.dot(high, table_low, preferred_element_type=F32)
-        + jnp.dot(low, table_high, preferred_element_type=F32)
-    )
-    row_real = response[:stations, :GRID]
-    row_imag = response[:stations, GRID:]
-    first = row // split * (split * share)
-    upper = first >= LANES
-    turn = lax.rem(2 * LANES - first, LANES)
-    column = response[stations:]
-    col_real = pltpu.roll(
-        jnp.where(upper, column[:, LANES : 2 * LANES], column[:, :LANES]), turn, 1
-    )
-    col_imag = pltpu.roll(
-        jnp.where(upper, column[:, 3 * LANES :], column[:, 2 * LANES : 3 * LANES]), turn, 1
-    )
-
-    for m in range(share * split):
-        c_real = col_real[:, m : m + 1]
-        c_imag = col_imag[:, m : m + 1]
-        beam_real = c_real * row_real - c_imag * row_imag
-        beam_imag = c_real * row_imag + c_imag * row_real
-        exact_ref[m, 0] = beam_real
-        exact_ref[m, 1] = beam_imag
-        beam_ref[m, :stations] = beam_imag.astype(BF16)
-        beam_ref[m, stations:] = beam_real.astype(BF16)
-        sum_real = jnp.dot(corr_real, beam_ref[m, stations:], preferred_element_type=F32)
-        sum_imag = jnp.dot(corr_both, beam_ref[m], preferred_element_type=F32)
-        total = exact_ref[m, 0] * sum_real + exact_ref[m, 1] * sum_imag
-        power_ref[m : m + 1, :] = jnp.sum(total, axis=0, keepdims=True) * scale
+    corr_ref[stations:] = lax.dot_general(both, both, outer, preferred_element_type=F32).astype(BF16)
+    turned = lax.dot_general(real, imag, outer, preferred_element_type=F32)
+    turned -= lax.dot_general(imag, real, outer, preferred_element_type=F32)
+    corr_ref[:stations] = (2.0 * turned).astype(BF16)
+
+    extra = gathered_ref[:, 2 * samples :].astype(F32).T
+    high, low, first = extra[: 2 * taps], extra[2 * taps : 4 * taps], extra[4 * taps : 4 * taps + 2]
+    row_high, row_low = spread(first[:1], high[:taps], low[:taps])
+    col_high, col_low = spread(first[1:], high[taps:], low[taps:])
+    rows_ref[...] = respond(tables_ref[...], row_high, row_low)
+    base = pl.multiple_of(row // split * columns, columns)
+    column_cos = respond(tables_ref[pl.ds(base, columns), :], col_high, col_low)
+    column_sin = respond(tables_ref[pl.ds(GRID + base, columns), :], col_high, col_low)
+
+    slots = ((beam_a, exact_a), (beam_b, exact_b))
+
+    group = beam_a.shape[0] // GRID
+
+    def build(step):
+        beam, exact = slots[step % 2]
+        r_real, r_imag = rows_ref[:GRID], rows_ref[GRID:]
+        for j in range(group):
+            m = step * group + j
+            lines = slice(j * GRID, (j + 1) * GRID)
+            c_real, c_imag = column_cos[m : m + 1], column_sin[m : m + 1]
+            beam_real = c_real * r_real - c_imag * r_imag
+            beam_imag = c_real * r_imag + c_imag * r_real
+            exact[0, lines] = beam_real
+            exact[1, lines] = beam_imag
+            beam[lines, :stations] = beam_real.astype(BF16)
+            beam[lines, stations:] = beam_imag.astype(BF16)
+
+    build(0)
+    steps = columns // group
+    for step in range(steps):
+        beam, exact = slots[step % 2]
+        sum_real = jnp.dot(beam[:, :stations], corr_ref[stations:], preferred_element_type=F32)
+        sum_imag = jnp.dot(beam[...], corr_ref[...], preferred_element_type=F32)
+        if step + 1 < steps:
+            build(step + 1)
+        total = exact[0] * sum_real + exact[1] * sum_imag
+        power = jnp.sum(total, axis=1, keepdims=True) * scale
+        for j in range(group):
+            m = step * group + j
+            column_ref[:, m : m + 1] = power[j * GRID : (j + 1) * GRID]
+    power = column_ref[...].T
     weights = weight_ref[...]
     for peer in range(peers):
         own = weights[:, peer * per_peer : (peer + 1) * per_peer]
@@ -135,7 +146,7 @@
             block = peer * split + side
             for m in range(share):
                 column = side * share + m
-                send_ref[block, :, m * GRID : (m + 1) * GRID] = power_ref[column : column + 1, :]
+                send_ref[block, :, m * GRID : (m + 1) * GRID] = power[column : column + 1, :]
             send_ref[block, :, share * GRID :] = own
 
 
@@ -186,17 +197,19 @@
 
 def imaged(gathered, tables, weight, peers, taps, share, split, scale, row_of, interpret=False):
     stations = gathered.shape[0]
-    columns = share * split
     return pl.pallas_call(
         functools.partial(image_kernel, taps, share, split, scale, row_of),
         out_shape=jax.ShapeDtypeStruct((peers * split, 1, share * GRID + LANES), F32),
         in_specs=[vmem()] * 3,
         out_specs=vmem(),
         scratch_shapes=[
-            pltpu.VMEM((stations, LANES), F32),
-            pltpu.VMEM((columns, 2 * stations, GRID), BF16),
-            pltpu.VMEM((columns, 2, stations, GRID), F32),
-            pltpu.VMEM((columns, GRID), F32),
+            pltpu.VMEM((2 * stations, stations), BF16),
+            pltpu.VMEM((2 * GRID, stations), F32),
+            pltpu.VMEM((GROUP * GRID, 2 * stations), BF16),
+            pltpu.VMEM((GROUP * GRID, 2 * stations), BF16),
+            pltpu.VMEM((2, GROUP * GRID, stations), F32),
+            pltpu.VMEM((2, GROUP * GRID, stations), F32),
+            pltpu.VMEM((GRID, LANES), F32),
         ],
         compiler_params=pltpu.CompilerParams(vmem_limit_bytes=32 << 20),
         name="image",

time: 50.5 us -> 49.5 us (0.980)
  Pallas kernels: 6.08 us -> 5.1 us
    pallas_call x1, Pallas kernels: 4.18 us -> 3.21 us  [imaged(): pl.pallas_call(functools.partial(image_kernel, taps, share, split, scale,...]
where the time goes in v5:
time: 49.5 us; the launch traced here: 49.3 us
  blocking collectives  43.5 us (88%)
  Pallas kernels  5.1 us (10%)
  between operations  0.66 us (1%)
    all_to_all x1, blocking collectives, on_device(): gathered = lax.all_to_all(send, 'row', 0, 0, tiled=True)  27.2 us
    all_to_all x1, blocking collectives, on_device(): lax.all_to_all(weighted, ('chan', 'row'), 0, 0, axis_index_groups=groups,...  16.4 us
    pallas_call x1, Pallas kernels, imaged(): pl.pallas_call(functools.partial(image_kernel, taps, share, split, scale,...  3.21 us
    pallas_call x1, Pallas kernels, packed(): pl.pallas_call(functools.partial(pack_kernel, peers, split), out_shape=(j...  1 us

profile of v5, /device:TPU:1, one launch (start us, length us, event | category | flops | bytes accessed | tf_op | source)
XLA Modules:
  0.0 49.3 jit_solution(10342538941855380389)
XLA Ops:
  0.6 1.0 %pack.1 = (bf16[32,8,1152]{2,1,0:T(8,128)(2,1)S(1)}, f32[1,16]{1,0:T(1,128)S(1)}) custom-call(bf16[8,2,1024]{2,1,0:T(2,128)(2,1)} %bitcast.12, f32[2,4,8]{2,1,0:T(4,128)} %bitcast.13, s32[2,8]{1,0:T(2,128)} %bitcast.14, f32[1,16]{1,0:T(1,128)} %bitcast.15), custom_call_target="tpu_custom_call" | custom-call | tf_op jit(solution)/shard_map/pack/pallas_call | solution.py:178
  1.6 0.0 copy-start
  1.7 27.2 %all_to_all.10 = bf16[32,8,1152]{2,1,0:T(8,128)(2,1)S(1)} all-to-all(bf16[32,8,1152]{2,1,0:T(8,128)(2,1)S(1)} %get-tuple-element.6), channel_id=1, replica_groups=mesh['chan'=8,'row'=32] {'row'}, dimensions={0} | all-to-all | bytes 1179648 | tf_op jit(solution)/shard_map/all_to_all | solution.py:246
  28.8 0.0 copy-done
  28.8 3.2 %image.1 = f32[16,1,2176]{2,1,0:T(1,128)S(1)} custom-call(bf16[256,1152]{1,0:T(8,128)(2,1)S(1)} %bitcast.11, bf16[512,512]{1,0:T(8,128)(2,1)S(1)} %copy-done, f32[1,16]{1,0:T(1,128)S(1)} %get-tuple-element.7.weight_ref), custom_call_target="tpu_custom_call" | custom-call | tf_op jit(solution)/shard_map/image/pallas_call | solution.py:200
  32.0 16.4 %all_to_all.11.parts_ref = f32[16,1,2176]{2,1,0:T(1,128)S(1)} all-to-all(f32[16,1,2176]{2,1,0:T(1,128)S(1)} %image.1), channel_id=1, replica_groups={{0,1,32,33,64,65,96,97,128,129,160,161,192,193,224,225},{2,3,34,35,66,6..., dimensions={0} | all-to-all | bytes 278528 | tf_op jit(solution)/shard_map/all_to_all | solution.py:256
  48.4 0.9 %finish.1 = (f32[8,256]{1,0:T(8,128)}, f32[16,256]{1,0:T(8,128)}) custom-call(f32[16,1,2176]{2,1,0:T(1,128)S(1)} %all_to_all.11.parts_ref), custom_call_target="tpu_custom_call" | custom-call | tf_op jit(solution)/shard_map/finish/pallas_call | solution.py:221
Async XLA Ops:
  1.6 27.2 %copy-start = (bf16[512,512]{1,0:T(8,128)(2,1)S(1)}, bf16[512,512]{1,0:T(8,128)(2,1)}, u32[]{:S(2)}) copy-start(bf16[512,512]{1,0:T(8,128)(2,1)} %constant.2.clone.tables_ref) | copy-start | bytes 1572868

commit v6 on v5

--- a/solution.py
+++ b/solution.py
@@ -11,7 +11,10 @@
 
 GRID = 256
 LANES = 128
-SPLIT = 2
+DEPTH = 8
+SPLIT_X = 2
+SPLIT_Z = 2
+SPLIT = SPLIT_X * SPLIT_Z
 GROUP = 2
 BF16 = jnp.bfloat16
 F32 = jnp.float32
@@ -24,6 +27,15 @@
     high = exact.astype(BF16)
     low = (exact - high.astype(np.float32)).astype(BF16)
     return np.concatenate([high, low], axis=1)
+
+
+def side_of(row):
+    return row // DEPTH % SPLIT_X * SPLIT_Z + row % DEPTH % SPLIT_Z
+
+
+def neighbours(row):
+    x, z = row // DEPTH // SPLIT_X * SPLIT_X, row % DEPTH // SPLIT_Z * SPLIT_Z
+    return [(x + i) * DEPTH + z + j for i in range(SPLIT_X) for j in range(SPLIT_Z)]
 
 
 def rounded(values):
@@ -52,7 +64,7 @@
     real = volt_ref[:, 0, :]
     imag = volt_ref[:, 1, :]
     for peer in range(peers):
-        start = (peer % split) * part
+        start = side_of(peer) * part
         out_ref[peer, :, :part] = real[:, start : start + part]
         out_ref[peer, :, part : 2 * part] = imag[:, start : start + part]
         out_ref[peer, :, 2 * part :] = extra
@@ -102,9 +114,11 @@
     row_high, row_low = spread(first[:1], high[:taps], low[:taps])
     col_high, col_low = spread(first[1:], high[taps:], low[taps:])
     rows_ref[...] = respond(tables_ref[...], row_high, row_low)
-    base = pl.multiple_of(row // split * columns, columns)
-    column_cos = respond(tables_ref[pl.ds(base, columns), :], col_high, col_low)
-    column_sin = respond(tables_ref[pl.ds(GRID + base, columns), :], col_high, col_low)
+    run = share * SPLIT_Z
+    bases = [pl.multiple_of(first * share, run) for first in neighbours(row)[::SPLIT_Z]]
+    mine = [tables_ref[pl.ds(part + base, run), :] for part in (0, GRID) for base in bases]
+    column = respond(jnp.concatenate(mine, axis=0), col_high, col_low)
+    column_cos, column_sin = column[:columns], column[columns:]
 
     slots = ((beam_a, exact_a), (beam_b, exact_b))
 
@@ -129,10 +143,13 @@
     for step in range(steps):
         beam, exact = slots[step % 2]
         sum_real = jnp.dot(beam[:, :stations], corr_ref[stations:], preferred_element_type=F32)
+        product = exact[0] * sum_real
+        total = product[:, :LANES] + product[:, LANES:]
         sum_imag = jnp.dot(beam[...], corr_ref[...], preferred_element_type=F32)
         if step + 1 < steps:
             build(step + 1)
-        total = exact[0] * sum_real + exact[1] * sum_imag
+        product = exact[1] * sum_imag
+        total += product[:, :LANES] + product[:, LANES:]
         power = jnp.sum(total, axis=1, keepdims=True) * scale
         for j in range(group):
             m = step * group + j
@@ -250,8 +267,9 @@
         lambda: lax.axis_index("row"),
     )
     groups = [
-        [c * rows + first + side for c in range(channels) for side in range(SPLIT)]
-        for first in range(0, rows, SPLIT)
+        [c * rows + near for c in range(channels) for near in neighbours(row)]
+        for row in range(rows)
+        if side_of(row) == 0
     ]
     parts = lax.all_to_all(
         weighted, ("chan", "row"), 0, 0, axis_index_groups=groups, tiled=True

time: 49.5 us -> 47.9 us (0.968)
  blocking collectives: 43.5 us -> 39.7 us
  Pallas kernels: 5.1 us -> 7.34 us
    all_to_all x1, blocking collectives: 27.2 us -> 21.9 us  [on_device(): gathered = lax.all_to_all(send, 'row', 0, 0, tiled=True)]
    pallas_call x1, Pallas kernels: 3.21 us -> 5.22 us  [imaged(): pl.pallas_call(functools.partial(image_kernel, taps, share, split, scale,...]
    all_to_all x1, blocking collectives: 16.4 us -> 17.8 us  [on_device(): lax.all_to_all(weighted, ('chan', 'row'), 0, 0, axis_index_groups=groups,...]
where the time goes in v6:
time: 47.9 us; the launch traced here: 47.7 us
  blocking collectives  39.7 us (83%)
  Pallas kernels  7.34 us (15%)
  between operations  0.66 us (1%)
    all_to_all x1, blocking collectives, on_device(): gathered = lax.all_to_all(send, 'row', 0, 0, tiled=True)  21.9 us
    all_to_all x1, blocking collectives, on_device(): lax.all_to_all(weighted, ('chan', 'row'), 0, 0, axis_index_groups=groups,...  17.8 us
    pallas_call x1, Pallas kernels, imaged(): pl.pallas_call(functools.partial(image_kernel, taps, share, split, scale,...  5.22 us
    pallas_call x1, Pallas kernels, finished(): pl.pallas_call(functools.partial(finish_kernel, split, channel_of), out_s...  1.07 us
    pallas_call x1, Pallas kernels, packed(): pl.pallas_call(functools.partial(pack_kernel, peers, split), out_shape=(j...  1.05 us

profile of v6, /device:TPU:1, one launch (start us, length us, event | category | flops | bytes accessed | tf_op | source)
XLA Modules:
  0.0 47.7 jit_solution(7736888898886426085)
XLA Ops:
  0.6 0.0 copy-start
  0.6 1.0 %pack.1 = (bf16[32,8,640]{2,1,0:T(8,128)(2,1)S(1)}, f32[1,16]{1,0:T(1,128)S(1)}) custom-call(bf16[8,2,1024]{2,1,0:T(2,128)(2,1)} %bitcast.12, f32[2,4,8]{2,1,0:T(4,128)} %bitcast.13, s32[2,8]{1,0:T(2,128)} %bitcast.14, f32[1,16]{1,0:T(1,128)} %bitcast.15), custom_call_target="tpu_custom_call" | custom-call | tf_op jit(solution)/shard_map/pack/pallas_call | solution.py:195
  1.7 21.9 %all_to_all.10 = bf16[32,8,640]{2,1,0:T(8,128)(2,1)S(1)} all-to-all(bf16[32,8,640]{2,1,0:T(8,128)(2,1)S(1)} %get-tuple-element.6), channel_id=1, replica_groups=mesh['chan'=8,'row'=32] {'row'}, dimensions={0} | all-to-all | bytes 655360 | tf_op jit(solution)/shard_map/all_to_all | solution.py:263
  23.6 0.0 copy-done
  23.6 5.2 %image.1 = f32[32,1,2176]{2,1,0:T(1,128)S(1)} custom-call(bf16[256,640]{1,0:T(8,128)(2,1)S(1)} %bitcast.11, bf16[512,512]{1,0:T(8,128)(2,1)S(1)} %copy-done, f32[1,16]{1,0:T(1,128)S(1)} %get-tuple-element.7.weight_ref), custom_call_target="tpu_custom_call" | custom-call | tf_op jit(solution)/shard_map/image/pallas_call | solution.py:217
  28.8 17.8 %all_to_all.11.parts_ref = f32[32,1,2176]{2,1,0:T(1,128)S(1)} all-to-all(f32[32,1,2176]{2,1,0:T(1,128)S(1)} %image.1), channel_id=1, replica_groups={{0,1,8,9,32,33,40,41,64,65,72,73,96,97,104,105,128,129,136,137,160,161,..., dimensions={0} | all-to-all | bytes 557056 | tf_op jit(solution)/shard_map/all_to_all | solution.py:274
  46.6 1.1 %finish.1 = (f32[8,256]{1,0:T(8,128)}, f32[16,256]{1,0:T(8,128)}) custom-call(f32[32,1,2176]{2,1,0:T(1,128)S(1)} %all_to_all.11.parts_ref), custom_call_target="tpu_custom_call" | custom-call | tf_op jit(solution)/shard_map/finish/pallas_call | solution.py:238
Async XLA Ops:
  0.6 22.9 %copy-start = (bf16[512,512]{1,0:T(8,128)(2,1)S(1)}, bf16[512,512]{1,0:T(8,128)(2,1)}, u32[]{:S(2)}) copy-start(bf16[512,512]{1,0:T(8,128)(2,1)} %constant.2.clone.tables_ref) | copy-start | bytes 1572868

commit v7 on v6

--- a/solution.py
+++ b/solution.py
@@ -95,7 +95,8 @@
                  corr_ref, rows_ref, beam_a, beam_b, exact_a, exact_b, column_ref):
     stations = gathered_ref.shape[0]
     samples = (gathered_ref.shape[1] - LANES) // 2
-    peers = send_ref.shape[0] // split
+    depth = GRID // LANES * share + 1
+    peers = send_ref.shape[0] // (depth * split)
     per_peer = weight_ref.shape[1] // peers
     columns = share * split
     row = row_of()
@@ -160,29 +161,35 @@
         own = weights[:, peer * per_peer : (peer + 1) * per_peer]
         own = jnp.concatenate([own, jnp.zeros((1, LANES - per_peer), F32)], axis=1)
         for side in range(split):
-            block = peer * split + side
-            for m in range(share):
-                column = side * share + m
-                send_ref[block, :, m * GRID : (m + 1) * GRID] = power[column : column + 1, :]
-            send_ref[block, :, share * GRID :] = own
+            start = (peer * split + side) * depth
+            for half in range(GRID // LANES):
+                lines = power[side * share : (side + 1) * share, half * LANES : (half + 1) * LANES]
+                send_ref[start + half * share : start + (half + 1) * share, :] = lines
+            send_ref[start + depth - 1 : start + depth, :] = own
 
 
 def finish_kernel(split, channel_of, parts_ref, power_ref, maps_ref):
     share = power_ref.shape[0]
     per_peer = maps_ref.shape[0] // share
+    halves = GRID // LANES
+    depth = halves * share + 1
     channel = channel_of()
-    blocks = parts_ref.shape[0]
-    parts = parts_ref[:, 0, :]
-    source = lax.broadcasted_iota(jnp.int32, (blocks, 1), 0) // split
-    mask = jnp.where(source == channel, 1.0, 0.0)
-    weights = parts[:, share * GRID :]
-    factors = [mask] + [weights[:, q : q + 1] for q in range(per_peer)]
-    for m in range(share):
-        block = parts[:, m * GRID : (m + 1) * GRID]
-        power_ref[m : m + 1, :] = jnp.sum(block * factors[0], axis=0, keepdims=True)
+    blocks = parts_ref.shape[0] // depth
+    power = jnp.zeros((halves * share, LANES), F32)
+    maps = [power] * per_peer
+    for block in range(blocks):
+        start = block * depth
+        part = parts_ref[start : start + depth - 1, :]
+        weights = parts_ref[start + depth - 1 : start + depth, :]
+        power += jnp.where(channel == block // split, part, 0.0)
         for q in range(per_peer):
-            place = q * share + m
-            maps_ref[place : place + 1, :] = jnp.sum(block * factors[1 + q], axis=0, keepdims=True)
+            maps[q] += part * weights[:, q : q + 1]
+    for half in range(halves):
+        lanes = slice(half * LANES, (half + 1) * LANES)
+        lines = slice(half * share, (half + 1) * share)
+        power_ref[:, lanes] = power[lines]
+        for q in range(per_peer):
+            maps_ref[q * share : (q + 1) * share, lanes] = maps[q][lines]
 
 
 def vmem():
@@ -216,7 +223,7 @@
     stations = gathered.shape[0]
     return pl.pallas_call(
         functools.partial(image_kernel, taps, share, split, scale, row_of),
-        out_shape=jax.ShapeDtypeStruct((peers * split, 1, share * GRID + LANES), F32),
+        out_shape=jax.ShapeDtypeStruct((peers * split * (share * GRID // LANES + 1), LANES), F32),
         in_specs=[vmem()] * 3,
         out_specs=vmem(),
         scratch_shapes=[
@@ -271,9 +278,11 @@
         for row in range(rows)
         if side_of(row) == 0
     ]
+    weighted = weighted.reshape(channels * SPLIT, 1, -1)
     parts = lax.all_to_all(
         weighted, ("chan", "row"), 0, 0, axis_index_groups=groups, tiled=True
     )
+    parts = parts.reshape(-1, LANES)
     power, maps = finished(parts, share, weight.shape[1] // channels, SPLIT, lambda: lax.axis_index("chan"))
     maps = maps.reshape(-1, share, GRID)
     return jnp.transpose(power[None], (0, 2, 1)), jnp.transpose(maps, (0, 2, 1))

time: 47.9 us -> 47.5 us (level)
  no operation moved by 1% of the time
where the time goes in v7:
time: 47.5 us; the launch traced here: 47.3 us
  blocking collectives  39.7 us (84%)
  Pallas kernels  6.99 us (15%)
  between operations  0.65 us (1%)
    all_to_all x1, blocking collectives, on_device(): gathered = lax.all_to_all(send, 'row', 0, 0, tiled=True)  21.9 us
    all_to_all x1, blocking collectives, on_device(): lax.all_to_all(weighted, ('chan', 'row'), 0, 0, axis_index_groups=groups,...  17.8 us
    pallas_call x1, Pallas kernels, imaged(): pl.pallas_call(functools.partial(image_kernel, taps, share, split, scale,...  5.18 us
    pallas_call x1, Pallas kernels, packed(): pl.pallas_call(functools.partial(pack_kernel, peers, split), out_shape=(j...  1.05 us

profile of v7, /device:TPU:1, one launch (start us, length us, event | category | flops | bytes accessed | tf_op | source)
XLA Modules:
  0.0 47.3 jit_solution(15673875117925785805)
XLA Ops:
  0.6 0.0 copy-start
  0.6 1.0 %pack.1 = (bf16[32,8,640]{2,1,0:T(8,128)(2,1)S(1)}, f32[1,16]{1,0:T(1,128)S(1)}) custom-call(bf16[8,2,1024]{2,1,0:T(2,128)(2,1)} %bitcast.16, f32[2,4,8]{2,1,0:T(4,128)} %bitcast.17, s32[2,8]{1,0:T(2,128)} %bitcast.18, f32[1,16]{1,0:T(1,128)} %bitcast.19), custom_call_target="tpu_custom_call" | custom-call | tf_op jit(solution)/shard_map/pack/pallas_call | solution.py:202
  1.7 21.9 %all_to_all.10 = bf16[32,8,640]{2,1,0:T(8,128)(2,1)S(1)} all-to-all(bf16[32,8,640]{2,1,0:T(8,128)(2,1)S(1)} %get-tuple-element.6), channel_id=1, replica_groups=mesh['chan'=8,'row'=32] {'row'}, dimensions={0} | all-to-all | bytes 655360 | tf_op jit(solution)/shard_map/all_to_all | solution.py:270
  23.6 0.0 copy-done
  23.6 5.2 %image.1 = f32[544,128]{1,0:T(8,128)S(1)} custom-call(bf16[256,640]{1,0:T(8,128)(2,1)S(1)} %bitcast.13, bf16[512,512]{1,0:T(8,128)(2,1)S(1)} %copy-done, f32[1,16]{1,0:T(1,128)S(1)} %get-tuple-element.7.weight_ref), custom_call_target="tpu_custom_call" | custom-call | tf_op jit(solution)/shard_map/image/pallas_call | solution.py:224
  28.7 17.8 %all_to_all.11 = f32[32,1,2176]{2,1,0:T(1,128)S(1)} all-to-all(f32[32,1,2176]{2,1,0:T(1,128)S(1)} %bitcast.14), channel_id=1, replica_groups={{0,1,8,9,32,33,40,41,64,65,72,73,96,97,104,105,128,129,136,137,160,161,..., dimensions={0} | all-to-all | bytes 557056 | tf_op jit(solution)/shard_map/all_to_all | solution.py:282
  46.6 0.8 %finish.1 = (f32[8,256]{1,0:T(8,128)}, f32[16,256]{1,0:T(8,128)}) custom-call(f32[544,128]{1,0:T(8,128)S(1)} %bitcast.15), custom_call_target="tpu_custom_call" | custom-call | tf_op jit(solution)/shard_map/finish/pallas_call | solution.py:245
Async XLA Ops:
  0.6 22.9 %copy-start = (bf16[512,512]{1,0:T(8,128)(2,1)S(1)}, bf16[512,512]{1,0:T(8,128)(2,1)}, u32[]{:S(2)}) copy-start(bf16[512,512]{1,0:T(8,128)(2,1)} %constant.2.clone.tables_ref) | copy-start | bytes 1572868

commit v8 on v7

--- a/solution.py
+++ b/solution.py
@@ -60,14 +60,22 @@
         turn_ref[axis * taps : (axis + 1) * taps, :stations] = high
         turn_ref[(2 + axis) * taps : (3 + axis) * taps, :stations] = values - high
     turn_ref[4 * taps : 4 * taps + 2, :stations] = foot_ref[...].astype(F32)
-    extra = turn_ref[...].T[:stations].astype(BF16)
-    real = volt_ref[:, 0, :]
-    imag = volt_ref[:, 1, :]
+    lines = []
+    for start, stop in ((0, 4 * taps), (4 * taps, 4 * taps + 2)):
+        line = turn_ref[start : start + 1]
+        for k in range(start + 1, stop):
+            line = line + pltpu.roll(turn_ref[k : k + 1], (k - start) * stations, 1)
+        lines.append(line)
+    extra = jnp.concatenate(lines, axis=0).astype(BF16)
+    values = (volt_ref[:, 0, :], volt_ref[:, 1, :])
+    depth = out_ref.shape[0] // peers
     for peer in range(peers):
-        start = side_of(peer) * part
-        out_ref[peer, :, :part] = real[:, start : start + part]
-        out_ref[peer, :, part : 2 * part] = imag[:, start : start + part]
-        out_ref[peer, :, 2 * part :] = extra
+        line = peer * depth
+        for value in values:
+            for start in range(side_of(peer) * part, (side_of(peer) + 1) * part, LANES):
+                out_ref[line : line + stations, :] = value[:, start : start + LANES]
+                line += stations
+        out_ref[line : line + 2, :] = extra
 
 
 def spread(first, high, low):
@@ -91,27 +99,48 @@
     )
 
 
-def image_kernel(taps, share, split, scale, row_of, gathered_ref, tables_ref, weight_ref, send_ref,
-                 corr_ref, rows_ref, beam_a, beam_b, exact_a, exact_b, column_ref):
-    stations = gathered_ref.shape[0]
-    samples = (gathered_ref.shape[1] - LANES) // 2
+def image_kernel(taps, share, split, scale, row_of, gathered_ref, tail_ref, tables_ref, weight_ref, send_ref,
+                 corr_ref, rows_ref, beam_a, beam_b, exact_a, exact_b, column_ref, volts_ref):
+    sources = tail_ref.shape[0]
+    local = LANES // (4 * taps)
+    stations = sources * local
+    lines = gathered_ref.shape[0] // sources
+    tiles = (lines - 2) // local // 2
+    for source in range(sources):
+        for tile in range(2 * tiles):
+            start = source * lines + tile * local
+            volts_ref[source * local : (source + 1) * local, tile * LANES : (tile + 1) * LANES] = (
+                gathered_ref[start : start + local, :]
+            )
+    samples = tiles * LANES
     depth = GRID // LANES * share + 1
     peers = send_ref.shape[0] // (depth * split)
     per_peer = weight_ref.shape[1] // peers
     columns = share * split
     row = row_of()
 
-    both = gathered_ref[:, : 2 * samples]
-    real = gathered_ref[:, :samples]
-    imag = gathered_ref[:, samples : 2 * samples]
+    both = volts_ref[...]
+    real = volts_ref[:, :samples]
+    imag = volts_ref[:, samples:]
     outer = (((1,), (1,)), ((), ()))
     corr_ref[stations:] = lax.dot_general(both, both, outer, preferred_element_type=F32).astype(BF16)
     turned = lax.dot_general(real, imag, outer, preferred_element_type=F32)
     turned -= lax.dot_general(imag, real, outer, preferred_element_type=F32)
     corr_ref[:stations] = (2.0 * turned).astype(BF16)
 
-    extra = gathered_ref[:, 2 * samples :].astype(F32).T
-    high, low, first = extra[: 2 * taps], extra[2 * taps : 4 * taps], extra[4 * taps : 4 * taps + 2]
+    source = lax.broadcasted_iota(jnp.int32, (sources, stations), 0)
+    station = lax.broadcasted_iota(jnp.int32, (sources, stations), 1)
+    expand = jnp.where(station // local == source, 1.0, 0.0).astype(BF16)
+    place = lax.broadcasted_iota(jnp.int32, (LANES, stations), 0) % local
+    wanted = place == lax.broadcasted_iota(jnp.int32, (LANES, stations), 1) % local
+    extras = []
+    for part in range(2):
+        spots = lax.dot_general(
+            tail_ref[:, tail_ref.shape[1] - 1, part, :], expand, (((0,), (0,)), ((), ())), preferred_element_type=F32
+        )
+        spots = jnp.where(wanted, spots, 0.0).reshape(LANES // local, local, stations)
+        extras.append(jnp.sum(spots, axis=1))
+    high, low, first = extras[0][: 2 * taps], extras[0][2 * taps :], extras[1][:2]
     row_high, row_low = spread(first[:1], high[:taps], low[:taps])
     col_high, col_low = spread(first[1:], high[taps:], low[taps:])
     rows_ref[...] = respond(tables_ref[...], row_high, row_low)
@@ -202,7 +231,7 @@
     return pl.pallas_call(
         functools.partial(pack_kernel, peers, split),
         out_shape=(
-            jax.ShapeDtypeStruct((peers, stations, 2 * samples // split + LANES), BF16),
+            jax.ShapeDtypeStruct((peers * (stations * 2 * samples // split // LANES + 2), LANES), BF16),
             jax.ShapeDtypeStruct(gain.shape, F32),
         ),
         in_specs=[pl.BlockSpec(memory_space=pltpu.HBM)] * 4,
@@ -219,12 +248,14 @@
     )(*inputs)
 
 
-def imaged(gathered, tables, weight, peers, taps, share, split, scale, row_of, interpret=False):
-    stations = gathered.shape[0]
+def imaged(gathered, tail, tables, weight, peers, taps, share, split, scale, row_of, interpret=False):
+    sources = tail.shape[0]
+    stations = sources * (LANES // (4 * taps))
+    width = (gathered.shape[0] // sources - 2) * LANES // (stations // sources)
     return pl.pallas_call(
         functools.partial(image_kernel, taps, share, split, scale, row_of),
         out_shape=jax.ShapeDtypeStruct((peers * split * (share * GRID // LANES + 1), LANES), F32),
-        in_specs=[vmem()] * 3,
+        in_specs=[vmem()] * 4,
         out_specs=vmem(),
         scratch_shapes=[
             pltpu.VMEM((2 * stations, stations), BF16),
@@ -234,11 +265,12 @@
             pltpu.VMEM((2, GROUP * GRID, stations), F32),
             pltpu.VMEM((2, GROUP * GRID, stations), F32),
             pltpu.VMEM((GRID, LANES), F32),
+            pltpu.VMEM((stations, width), BF16),
         ],
         compiler_params=pltpu.CompilerParams(vmem_limit_bytes=32 << 20),
         name="image",
         interpret=interpret,
-    )(gathered, tables, weight)
+    )(gathered, tail, tables, weight)
 
 
 def finished(parts, share, per_peer, split, channel_of, interpret=False):
@@ -267,10 +299,11 @@
     volt = voltages.reshape(local_stations, 2, samples)
     kern = jnp.transpose(kernels, (1, 2, 0))
     send, weight = packed(volt, kern, footprint.T, cal_weight.T, rows, SPLIT)
-    gathered = lax.all_to_all(send, "row", 0, 0, tiled=True)
-    gathered = gathered.reshape(station_count, -1)
+    send = send.reshape(rows, -1, 2, LANES)
+    blocks = lax.all_to_all(send, "row", 0, 0, tiled=True)
+    gathered = blocks.reshape(-1, LANES)
     weighted = imaged(
-        gathered, tables, weight, channels, taps, share, SPLIT, scale,
+        gathered, blocks, tables, weight, channels, taps, share, SPLIT, scale,
         lambda: lax.axis_index("row"),
     )
     groups = [

time: 47.5 us -> 46.9 us (0.987)
  blocking collectives: 39.7 us -> 38.7 us
    all_to_all x1, blocking collectives: 17.8 us -> 17.3 us  [on_device(): lax.all_to_all(weighted, ('chan', 'row'), 0, 0, axis_index_groups=groups,...]
where the time goes in v8:
time: 46.9 us; the launch traced here: 46.7 us
  blocking collectives  38.7 us (83%)
  Pallas kernels  7.33 us (16%)
  between operations  0.65 us (1%)
    all_to_all x1, blocking collectives, on_device(): blocks = lax.all_to_all(send, 'row', 0, 0, tiled=True)  21.4 us
    all_to_all x1, blocking collectives, on_device(): lax.all_to_all(weighted, ('chan', 'row'), 0, 0, axis_index_groups=groups,...  17.3 us
    pallas_call x1, Pallas kernels, imaged(): pl.pallas_call(functools.partial(image_kernel, taps, share, split, scale,...  5.45 us
    pallas_call x1, Pallas kernels, packed(): pl.pallas_call(functools.partial(pack_kernel, peers, split), out_shape=(j...  1.12 us

profile of v8, /device:TPU:1, one launch (start us, length us, event | category | flops | bytes accessed | tf_op | source)
XLA Modules:
  0.0 46.7 jit_solution(7964011970423847356)
XLA Ops:
  0.6 0.0 copy-start
  0.6 1.1 %pack.1 = (bf16[1088,128]{1,0:T(8,128)(2,1)S(1)}, f32[1,16]{1,0:T(1,128)S(1)}) custom-call(bf16[8,2,1024]{2,1,0:T(2,128)(2,1)} %bitcast.18, f32[2,4,8]{2,1,0:T(4,128)} %bitcast.19, s32[2,8]{1,0:T(2,128)} %bitcast.20, f32[1,16]{1,0:T(1,128)} %bitcast.21), custom_call_target="tpu_custom_call" | custom-call | tf_op jit(solution)/shard_map/pack/pallas_call | solution.py:231
  1.8 21.4 %all_to_all.10.tail_ref = bf16[32,17,2,128]{3,2,1,0:T(2,128)(2,1)S(1)} all-to-all(bf16[32,17,2,128]{3,2,1,0:T(2,128)(2,1)S(1)} %bitcast.17), channel_id=1, replica_groups=mesh['chan'=8,'row'=32] {'row'}, dimensions={0} | all-to-all | bytes 557056 | tf_op jit(solution)/shard_map/all_to_all | solution.py:303
  23.2 0.0 copy-done
  23.2 5.5 %image.1 = f32[544,128]{1,0:T(8,128)S(1)} custom-call(bf16[1088,128]{1,0:T(8,128)(2,1)S(1)} %bitcast.14, bf16[32,17,2,128]{3,2,1,0:T(2,128)(2,1)S(1)} %all_to_all.10.tail_ref, bf16[512,512]{1,0:T(8,128)(2,1)S(1)} %copy-done, f32[1,16]{1,0:T(1,128)S(1)} %get-tuple-element.7.weight_ref), custom_call_target="tpu_custom_call" | custom-call | tf_op jit(solution)/shard_map/image/pallas_call | solution.py:255
  28.6 17.3 %all_to_all.11 = f32[32,1,2176]{2,1,0:T(1,128)S(1)} all-to-all(f32[32,1,2176]{2,1,0:T(1,128)S(1)} %bitcast.15), channel_id=1, replica_groups={{0,1,8,9,32,33,40,41,64,65,72,73,96,97,104,105,128,129,136,137,160,161,..., dimensions={0} | all-to-all | bytes 557056 | tf_op jit(solution)/shard_map/all_to_all | solution.py:315
  46.0 0.8 %finish.1 = (f32[8,256]{1,0:T(8,128)}, f32[16,256]{1,0:T(8,128)}) custom-call(f32[544,128]{1,0:T(8,128)S(1)} %bitcast.16), custom_call_target="tpu_custom_call" | custom-call | tf_op jit(solution)/shard_map/finish/pallas_call | solution.py:277
Async XLA Ops:
  0.6 22.6 %copy-start = (bf16[512,512]{1,0:T(8,128)(2,1)S(1)}, bf16[512,512]{1,0:T(8,128)(2,1)}, u32[]{:S(2)}) copy-start(bf16[512,512]{1,0:T(8,128)(2,1)} %constant.2.clone.tables_ref) | copy-start | bytes 1572868
